TPU v7x, 128 devices: a whole 4x4x4 slice. The times are simulated.
128 devices in a mesh: dev: 16 (over z_hi, y, core), ha: 8 (over z_lo, x).
Axes of the slice: x: 4, y: 4, z: 4 (z_hi: 2, z_lo: 2; z = z_hi * 2 + z_lo), core: 2. Of those that a mesh axis runs over, the one named last changes fastest.
Arguments:
- volume: bfloat16 [4, 128, 128, 512], P(None, 'dev', 'ha'), may hold values from -6 to 6
- w_first: bfloat16 [3, 3, 3, 4, 32], replicated, may hold values from -0.625 to 0.625
- w_second: bfloat16 [3, 3, 3, 32, 64], replicated, may hold values from -0.21875 to 0.21875
- w_third: bfloat16 [3, 3, 3, 64, 128], P(None, None, None, None, 'ha'), may hold values from -0.15625 to 0.15625
- cotangent: bfloat16 [128, 16, 16, 64], P('ha', 'dev'), may hold values from -6 to 6
Outputs:
- out_third: bfloat16 [128, 16, 16, 64], P('ha', 'dev')
- grad_first: float32 [3, 3, 3, 4, 32], replicated
- grad_second: float32 [3, 3, 3, 32, 64], replicated
- grad_third: float32 [3, 3, 3, 64, 128], P(None, None, None, None, 'ha')
All inputs are finite; a program needn't handle non-finite values.
Results may differ from a plain program's by a relative error of at most 0.0063.
Values may be sent and summed in bfloat16 or wider, within the bound.
A program may use at most 192 MiB of HBM per device.

v0:
```python
import math

import jax
import jax.numpy as jnp
from jax import lax
from jax.sharding import PartitionSpec as P


def shifted(block, axis, distance):
    devices = range(lax.axis_size(axis))
    route = [(i - distance, i) for i in devices if i - distance in devices]
    return lax.ppermute(block, axis, route)


def leaky_relu(values):
    return 0.3 * values + 0.175 * jax.nn.softplus(4.0 * values)


def leaky_slope(values):
    return 0.3 + 0.7 * jax.nn.sigmoid(4.0 * values)


def convolve(inputs, kernel, pad_depth, pad_height):
    return lax.conv_general_dilated(
        inputs[None],
        kernel,
        (2, 2, 2),
        [pad_depth, pad_height, (1, 0)],
        dimension_numbers=("NCDHW", "DHWIO", "NCDHW"),
        preferred_element_type=jnp.float32,
    )[0]


def weight_grad(inputs, delta, pad_depth, pad_height):
    result = lax.conv_general_dilated(
        inputs[:, None],
        delta[:, None],
        (1, 1, 1),
        [pad_depth, pad_height, (1, 0)],
        rhs_dilation=(2, 2, 2),
        dimension_numbers=("NCDHW", "OIDHW", "NCDHW"),
        preferred_element_type=jnp.float32,
    )
    return jnp.transpose(result, (2, 3, 4, 0, 1))


def input_grad(delta, kernel):
    flipped = jnp.flip(kernel, (0, 1, 2))
    return lax.conv_general_dilated(
        delta[None],
        flipped,
        (1, 1, 1),
        [(2, 2)] * 3,
        lhs_dilation=(2, 2, 2),
        dimension_numbers=("NCDHW", "DHWOI", "NCDHW"),
        preferred_element_type=jnp.float32,
    )[0]


def extend_depth(values):
    lower = shifted(values[:, -1:], "dev", 1)
    return jnp.concatenate([lower, values], 1)


def extend(values):
    deeper = extend_depth(values)
    beside = shifted(deeper[:, :, -1:], "ha", 1)
    return jnp.concatenate([beside, deeper], 2)


def retract_depth(grads):
    lower = shifted(grads[:, 0:1], "dev", -1)
    inner = grads[:, 1:]
    return inner.at[:, -1:].add(lower)


def retract(grads):
    beside = shifted(grads[:, :, 0:1].astype(jnp.bfloat16), "ha", -1).astype(jnp.float32)
    inner = grads[:, :, 1:]
    inner = inner.at[:, :, -1:].add(beside)
    return retract_depth(inner)


def local(volume, w_first, w_second, w_third, cotangent):
    depth_total = volume.shape[1] * lax.axis_size("dev")
    height_total = volume.shape[2] * lax.axis_size("ha")
    width_total = volume.shape[3]
    scale_first = 1.0 / math.sqrt(depth_total // 2 * (height_total // 2) * (width_total // 2))
    scale_second = 1.0 / math.sqrt(depth_total // 4 * (height_total // 4) * (width_total // 4))
    scale_third = 1.0 / math.sqrt(depth_total // 8 * (height_total // 8) * (width_total // 8))
    whole_first = extend(volume)
    pre_first = convolve(whole_first, w_first, (0, 0), (0, 0))
    act_first = leaky_relu(pre_first).astype(jnp.bfloat16)
    whole_second = extend(act_first)
    pre_second = convolve(whole_second, w_second, (0, 0), (0, 0))
    act_second = leaky_relu(pre_second).astype(jnp.bfloat16)
    deeper = extend_depth(act_second)
    all_rows = lax.all_gather(deeper, "ha", axis=2, tiled=True)
    pre_third = convolve(all_rows, w_third, (0, 0), (1, 0))
    out_third = leaky_relu(pre_third).astype(jnp.bfloat16)
    delta_third = (cotangent.astype(jnp.float32) * leaky_slope(pre_third)).astype(jnp.bfloat16)
    grad_third = lax.psum(weight_grad(all_rows, delta_third, (0, 0), (1, 0)), "dev") * scale_third
    partial_back = input_grad(delta_third, w_third)[:, :, 1:, 1:]
    summed_back = lax.psum_scatter(partial_back, "ha", scatter_dimension=2, tiled=True)
    back_second = retract_depth(summed_back)
    delta_second = (back_second * leaky_slope(pre_second)).astype(jnp.bfloat16)
    local_second = weight_grad(whole_second, delta_second, (0, 0), (0, 0))
    back_first = retract(input_grad(delta_second, w_second)[..., 1:])
    delta_first = (back_first * leaky_slope(pre_first)).astype(jnp.bfloat16)
    local_first = weight_grad(whole_first, delta_first, (0, 0), (0, 0))
    grad_first, grad_second = lax.psum((local_first, local_second), ("dev", "ha"))
    return (out_third, grad_first * scale_first, grad_second * scale_second, grad_third)


def solution(mesh):
    placed = (
        P(None, "dev", "ha", None),
        P(),
        P(),
        P(None, None, None, None, "ha"),
        P("ha", "dev", None, None),
    )
    return jax.shard_map(
        local,
        mesh=mesh,
        in_specs=placed,
        out_specs=(P("ha", "dev", None, None), P(), P(), P(None, None, None, None, "ha")),
        check_vma=False,
    )
```

profile of v0, /device:TPU:1, one launch (start us, length us, event | category | flops | bytes accessed | tf_op | source)
XLA Modules:
  0.0 800.9 jit_solution(4794022419760191605)
XLA Ops:
  7.2 0.9 slice.130
  8.1 4.6 collective-permute-start
  12.7 1.3 collective-permute-done
  14.0 1.1 constant_dynamic-update-slice_fusion
  15.2 3.1 collective-permute-start.1
  18.3 1.4 collective-permute-done.1
  19.7 1.3 fusion.27
  21.5 1.5 reshape.287
  22.9 10.8 %copy.123 = bf16[4,9,17,1,8,66]{4,0,5,2,1,3:T(4,128)(2,1)} copy(bf16[4,9,17,1,8,66]{5,4,2,1,0,3:T(8,128)(2,1)S(1)} %reshape.287) | data formatting | bytes 1292544 | tf_op jit(solution)/shard_map/conv_general_dilated | solution.py:24
  33.7 1.2 slice.159
  35.0 32.7 %fusion.3 = f32[4,8,8,33,32]{4,2,3,1,0:T(8,128)} fusion(bf16[3,3,3,4,32]{4,3,2,1,0:T(4,128)(2,1)S(1)} %copy-done.15, bf16[4,9,17,1,7,2]{4,0,5,2,1,3:T(4,128)(2,1)S(1)} %slice.159, bf16[4,9,17,1,8,66]{4,0,5,2,1,3:T(4,128)(2,1)} %copy.123), kind=kOutput, calls=%fused_computation.4 | convolution fusion | flops 60390144 | bytes 1751664 | tf_op jit(solution)/shard_map/conv_general_dilated | solution.py:24
  67.7 18.2 %copy.124 = f32[4,8,8,33,32]{3,4,2,1,0:T(8,128)} copy(f32[4,8,8,33,32]{4,2,3,1,0:T(8,128)} %fusion.3) | data formatting | bytes 2162688 | tf_op jit(solution)/shard_map/conv_general_dilated | solution.py:24
  85.9 5.1 select_multiply_fusion
  91.0 5.9 copy.126
  96.9 3.5 reshape.226
  100.4 8.6 %copy.125 = f32[4,8,8,33,32]{3,2,4,1,0:T(8,128)} copy(f32[4,8,8,33,32]{3,4,2,1,0:T(8,128)} %get-tuple-element.53) | data formatting | bytes 2162688 | tf_op jit(solution)/shard_map/mul | solution.py:16
  109.0 3.5 reshape.224
  113.2 5.1 collective-permute-start.2
  118.3 1.9 collective-permute-done.2
  120.2 4.0 collective-permute-start.3
  124.2 1.5 collective-permute-done.3
  125.7 1.0 fusion.43
  126.7 1.5 pad.8
  128.1 4.0 reshape.229
  132.1 4.5 copy.128
  136.7 1.0 slice.163
  137.7 3.7 broadcast_multiply_fusion.2
  143.1 5.2 collective-permute-start.4
  148.3 1.9 collective-permute-done.4
  150.5 0.9 copy.131
  151.5 48.0 %all-gather.2.cloned.1.call-done = bf16[64,3,32,128]{3,0,1,2:T(8,128)(2,1)} async-done(((bf16[64,3,4,128]{3,0,1,2:T(8,128)(2,1)}), bf16[64,3,32,128]{3,0,1,2:T(8,128)(2,1)}) %all-gather.2.cloned.1.call-update) | async-done | bytes 1572880 | tf_op jit(solution)/shard_map/all_gather | solution.py:98
  199.5 5.8 copy.132
  205.9 2.3 copy.134
  208.4 2.2 broadcast_multiply_fusion
  212.9 4.3 broadcast_select_fusion
  217.1 5.8 copy.143
  223.0 9.0 %reshape.251 = f32[3,33,1,144,64]{4,3,1,0,2:T(8,128)} reshape(f32[3,33,8,18,64]{4,3,2,1,0:T(8,128)} %copy.143) | data formatting | bytes 7299072 | tf_op jit(solution)/shard_map/conv_general_dilated | solution.py:49
  231.9 3.4 slice_bitcast_fusion
  235.3 3.7 slice.172
  239.1 6.2 copy.144
  245.3 56.0 %copy.151 = bf16[4,1,9,17,512]{0,1,4,3,2:T(2,128)(2,1)} copy(bf16[4,1,9,17,512]{4,3,2,0,1:T(8,128)(2,1)S(1)} %copy-done.8) | data formatting | bytes 1253376 | tf_op jit(solution)/shard_map/broadcast_in_dim | solution.py:36
  301.3 8.8 %copy.153 = bf16[32,1,5,9,256]{0,1,4,3,2:T(2,128)(2,1)} copy(bf16[32,1,5,9,256]{4,0,3,2,1:T(8,128)(2,1)S(1)} %copy-done.9) | data formatting | bytes 1474560 | tf_op jit(solution)/shard_map/broadcast_in_dim | solution.py:36
  310.6 10.5 %copy.156 = bf16[64,1,3,32,128]{0,1,4,3,2:T(2,128)(2,1)} copy(bf16[64,1,3,32,128]{4,0,2,3,1:T(8,128)(2,1)S(1)} %bitcast.160) | data formatting | bytes 3145728 | tf_op jit(solution)/shard_map/broadcast_in_dim | solution.py:36
  321.1 1.0 fusion.84
  322.3 8.7 %collective-permute-start.5 = (f32[64,1,4,128]{0,2,3,1:T(4,128)S(1)}, f32[64,1,4,128]{0,2,3,1:T(4,128)S(1)}, u32[]{:S(2)}, u32[]{:S(2)}) collective-permute-start(f32[64,1,4,128]{0,2,3,1:T(4,128)S(1)} %copy.168), channel_id=1, source_target_pairs={{8,0},{16,8},{24,16},{32,24},{40,32},{48,40},{56,48},{64,56},{72,6... | collective-permute-start | bytes 393224 | tf_op jit(solution)/shard_map/ppermute | solution.py:12
  331.0 15.7 %fusion.86 = f32[3,3,3,64,16]{3,4,2,1,0:T(8,128)} fusion(bf16[64,1,3,32,128]{0,1,4,3,2:T(2,128)(2,1)} %copy.156, bf16[16,1,1,16,64]{0,1,4,3,2:T(2,128)(2,1)S(1)} %copy.157), kind=kOutput, calls=%fused_computation.117 | convolution fusion | flops 55154688 | bytes 1716224 | tf_op jit(solution)/shard_map/transpose | solution.py:44
  348.5 7.4 broadcast_select_fusion.1
  355.9 8.4 %copy.150 = f32[5,9,8,34,32]{3,2,4,1,0:T(8,128)} copy(f32[5,9,8,34,32]{4,2,3,1,0:T(8,128)} %broadcast_select_fusion.1) | data formatting | bytes 3133440 | tf_op jit(solution)/shard_map/conv_general_dilated | solution.py:49
  364.3 4.2 reshape.258
  368.6 1.4 copy-done.6
  370.1 1.5 collective-permute-start.6
  371.7 14.7 %fusion.35 = f32[3,3,3,32,64]{4,3,2,1,0:T(8,128)} fusion(bf16[32,1,5,9,256]{0,1,4,3,2:T(2,128)(2,1)} %copy.153, bf16[64,1,2,4,128]{0,3,4,2,1:T(4,128)(2,1)S(1)} %fusion.97), kind=kOutput, calls=%fused_computation.49 | convolution fusion | flops 112951296 | bytes 1089536 | tf_op jit(solution)/shard_map/transpose | solution.py:44
  386.3 2.1 slice.178
  388.4 1.1 fusion.52
  390.3 2.2 collective-permute-start.7
  392.5 88.5 %all-reduce.5.cloned.1.call-done = f32[3,3,3,64,16]{3,4,2,1,0:T(8,128)} async-done(((f32[3,3,3,64,16]{3,4,2,1,0:T(8,128)}), f32[3,3,3,64,16]{3,4,2,1,0:T(8,128)}) %all-reduce.5.cloned.1.call-update) | async-done | bytes 110608 | tf_op jit(solution)/shard_map/psum | solution.py:102
  481.0 1.6 broadcast_multiply_fusion.5
  482.6 1.1 slice.181
  483.7 146.6 %all-reduce.3.cloned.1.call-done = f32[3,3,3,32,64]{4,3,2,1,0:T(8,128)} async-done(((f32[3,3,3,32,64]{4,3,2,1,0:T(8,128)}), f32[3,3,3,32,64]{4,3,2,1,0:T(8,128)}) %all-reduce.3.cloned.1.call-update) | async-done | bytes 221200 | tf_op jit(solution)/shard_map/psum | solution.py:111
  630.3 1.8 broadcast_multiply_fusion.4
  632.8 1.6 fusion.34
  634.4 7.2 copy.152
  641.7 87.7 %fusion.85 = f32[3,3,3,4,32]{4,3,2,1,0:T(4,128)S(1)} fusion(bf16[4,1,9,17,512]{0,1,4,3,2:T(2,128)(2,1)} %copy.151, bf16[32,1,4,8,256]{0,1,4,3,2:T(2,128)(2,1)} %copy.152), kind=kOutput, calls=%fused_computation.116 | convolution fusion | flops 56549376 | bytes 1164800 | tf_op jit(solution)/shard_map/transpose | solution.py:44
  729.4 63.8 %psum.21 = f32[3,3,3,4,32]{4,3,2,1,0:T(4,128)S(1)} all-reduce(f32[3,3,3,4,32]{4,3,2,1,0:T(4,128)S(1)} %fusion.85), channel_id=1, replica_groups=mesh['dev'=16,'ha'=8] {'dev','ha'}, use_global_device_ids=true, to_apply=%region_1.2 | all-reduce | flops 3456 | bytes 27648 | tf_op jit(solution)/shard_map/psum | solution.py:111
  (88 shorter events, 10.9 us)
Async XLA Ops:
  7.2 130.5 %copy-start = (bf16[3,3,3,32,64]{4,3,2,1,0:T(8,128)(2,1)S(1)}, bf16[3,3,3,32,64]{4,3,2,1,0:T(8,128)(2,1)}, u32[]{:S(2)}) copy-start(bf16[3,3,3,32,64]{4,3,2,1,0:T(8,128)(2,1)} %param.13) | copy-start | bytes 331780
  7.2 192.3 %all-gather.2.cloned.1.call-start = ((), (), s32[]{:S(2)}) async-start(), calls=%async_computation.1 | async-start | bytes 1769472 | tf_op jit(solution)/shard_map/all_gather | solution.py:98
  8.1 5.9 collective-permute-start
  15.2 4.5 collective-permute-start.1
  22.9 12.0 %copy-start.15 = (bf16[3,3,3,4,32]{4,3,2,1,0:T(4,128)(2,1)S(1)}, bf16[3,3,3,4,32]{4,3,2,1,0:T(4,128)(2,1)}, u32[]{:S(2)}) copy-start(bf16[3,3,3,4,32]{4,3,2,1,0:T(4,128)(2,1)} %param.12) | copy-start | bytes 20740
  67.7 18.2 %copy-start.14 = (pred[8,33]{1,0:T(8,128)(4,1)S(1)}, pred[8,33]{1,0:T(8,128)(4,1)}, u32[]{:S(2)}) copy-start(pred[8,33]{1,0:T(8,128)(4,1)} %constant.142) | copy-start | bytes 796
  100.4 12.1 %copy-start.2 = (f32[4,8,1,264,32]{3,4,1,0,2:T(8,128)}, f32[4,8,1,264,32]{3,4,1,0,2:T(8,128)S(1)}, u32[]{:S(2)}) copy-start(f32[4,8,1,264,32]{3,4,1,0,2:T(8,128)S(1)} %reshape.226) | copy-start | bytes 3244036
  113.2 7.1 collective-permute-start.2
  120.2 5.5 collective-permute-start.3
  132.1 5.5 copy-start.16
  141.6 0.8 copy-start.4
  143.1 7.1 collective-permute-start.4
  151.5 169.6 %reduce-scatter.2.cloned.1.call-start = ((), (), s32[]{:S(2)}) async-start(), calls=%async_computation.2 | async-start | bytes 3538944 | tf_op jit(solution)/shard_map/reduce_scatter | solution.py:104
  205.9 2.4 copy-start.10
  205.9 2.4 copy-start.17
  210.6 0.9 copy-start.11
  210.6 2.2 copy-start.13
  239.1 6.3 copy-start.8
  245.3 235.7 %all-reduce.5.cloned.1.call-start = ((), (), s32[]{:S(2)}) async-start(), calls=%async_computation.4 | async-start | bytes 442368 | tf_op jit(solution)/shard_map/psum | solution.py:102
  245.3 56.0 %copy-start.9 = (bf16[32,1,5,9,256]{4,0,3,2,1:T(8,128)(2,1)S(1)}, bf16[32,1,5,9,256]{4,0,3,2,1:T(8,128)(2,1)}, u32[]{:S(2)}) copy-start(bf16[32,1,5,9,256]{4,0,3,2,1:T(8,128)(2,1)} %get-tuple-element.54) | copy-start | bytes 2211844
  301.3 9.2 %copy-start.7 = (bf16[64,3,32,128]{3,0,1,2:T(8,128)(2,1)S(1)}, bf16[64,3,32,128]{3,0,1,2:T(8,128)(2,1)}, u32[]{:S(2)}) copy-start(bf16[64,3,32,128]{3,0,1,2:T(8,128)(2,1)} %all-gather.2.cloned.1.call-done) | copy-start | bytes 4718596
  322.2 24.9 %slice-start = ((f32[64,3,4,128]{3,0,1,2:T(8,128)}), f32[64,2,4,128]{3,0,1,2:T(8,128)S(1)}, s32[]{:S(2)}) async-start(f32[64,3,4,128]{3,0,1,2:T(8,128)} %reduce-scatter.2.cloned.1.call-done), calls=%async_computation.5 | async-start | bytes 524288 | tf_op jit(solution)/shard_map/slice | solution.py:73
  322.3 25.3 %copy-start.5 = (f32[2,4,8,17,64]{4,1,3,2,0:T(4,128)S(1)}, f32[2,4,8,17,64]{4,1,3,2,0:T(4,128)}, u32[]{:S(2)}) copy-start(f32[2,4,8,17,64]{4,1,3,2,0:T(4,128)} %copy-done.4) | copy-start | bytes 835588
  322.3 25.2 %collective-permute-start.5 = (f32[64,1,4,128]{0,2,3,1:T(4,128)S(1)}, f32[64,1,4,128]{0,2,3,1:T(4,128)S(1)}, u32[]{:S(2)}, u32[]{:S(2)}) collective-permute-start(f32[64,1,4,128]{0,2,3,1:T(4,128)S(1)} %copy.168), channel_id=1, source_target_pairs={{8,0},{16,8},{24,16},{32,24},{40,32},{48,40},{56,48},{64,56},{72,6... | collective-permute-start | bytes 393224 | tf_op jit(solution)/shard_map/ppermute | solution.py:12
  346.7 1.7 copy-start.12
  346.8 283.5 %all-reduce.3.cloned.1.call-start = ((), (), s32[]{:S(2)}) async-start(), calls=%async_computation.3 | async-start | bytes 884736 | tf_op jit(solution)/shard_map/psum | solution.py:111
  368.6 1.4 copy-start.6
  370.1 18.3 %collective-permute-start.6 = (bf16[32,5,1,256]{3,0,2,1:T(8,128)(2,1)S(1)}, bf16[32,5,1,256]{3,0,2,1:T(8,128)(2,1)S(1)}, u32[]{:S(2)}, u32[]{:S(2)}) collective-permute-start(bf16[32,5,1,256]{3,0,2,1:T(8,128)(2,1)S(1)} %slice.211), channel_id=1, source_target_pairs={{1,0},{2,1},{3,2},{4,3},{5,4},{6,5},{7,6},{9,8},{10,9},{11,10},{12... | collective-permute-start | bytes 245768 | tf_op jit(solution)/shard_map/ppermute | solution.py:12
  386.3 246.5 %copy-start.3 = (f32[4,8,1,264,32]{3,4,1,0,2:T(8,128)S(1)}, f32[4,8,1,264,32]{3,4,1,0,2:T(8,128)}, u32[]{:S(2)}) copy-start(f32[4,8,1,264,32]{3,4,1,0,2:T(8,128)} %copy-done.2) | copy-start | bytes 3244036
  390.3 241.9 %collective-permute-start.7 = (f32[32,1,8,256]{3,0,2,1:T(8,128)}, f32[32,1,8,256]{3,0,2,1:T(8,128)S(1)}, u32[]{:S(2)}, u32[]{:S(2)}) collective-permute-start(f32[32,1,8,256]{3,0,2,1:T(8,128)} %slice.183), channel_id=1, source_target_pairs={{8,0},{16,8},{24,16},{32,24},{40,32},{48,40},{56,48},{64,56},{72,6... | collective-permute-start | bytes 786440 | tf_op jit(solution)/shard_map/ppermute | solution.py:12
  641.7 152.2 %copy-start.1 = (bf16[3,3,3,32,64]{4,3,2,1,0:T(8,128)(2,1)S(1)}, bf16[3,3,3,32,64]{4,3,2,1,0:T(8,128)(2,1)}, u32[]{:S(2)}) copy-start(bf16[3,3,3,32,64]{4,3,2,1,0:T(8,128)(2,1)} %param.13) | copy-start | bytes 331780
Sparse Core Ops, SparseCore 0:
  151.6 47.8 all-gather.1
  245.4 47.8 reduce-scatter.1
  346.9 134.0 all-reduce.4
  486.2 144.0 all-reduce.2
where the time goes:
time: 810 us; the launch traced here: 801 us
  waiting for transfers between devices  291 us (36%)
  local copies, waits for them, and re-layouts  210 us (26%)
  matrix products  168 us (21%)
  blocking collectives  63.8 us (8%)
  starting transfers between devices  34.9 us (4%)
  other arithmetic  18 us (2%)
  between operations  14.9 us (2%)
    psum x1, waiting for transfers between devices, local(): lax.psum((local_first, local_second), ('dev', 'ha'))  147 us
    transpose x3, matrix products, weight_grad(): return jnp.transpose(result, (2, 3, 4, 0, 1))  118 us
    psum x1, waiting for transfers between devices, local(): lax.psum(weight_grad(all_rows, delta_third, (0, 0), (1, 0)), 'dev')  88.5 us
    broadcast_in_dim x3, local copies, waits for them, and re-layouts, weight_grad(): inputs[:, None]  75.3 us
    psum x1, blocking collectives, local(): lax.psum((local_first, local_second), ('dev', 'ha'))  63.8 us
    all_gather x1, waiting for transfers between devices, local(): all_rows = lax.all_gather(deeper, 'ha', axis=2, tiled=True)  48 us
    conv_general_dilated x9, local copies, waits for them, and re-layouts, convolve(): lax.conv_general_dilated(inputs[None], kernel, (2, 2, 2), [pad_depth, pad...  43.6 us
    conv_general_dilated x3, matrix products, convolve(): lax.conv_general_dilated(inputs[None], kernel, (2, 2, 2), [pad_depth, pad...  38.7 us
  transfers between devices with their start and end apart: 12, of which 8 were waited for; matrix products, arithmetic and copies ran while one was open for 17% of the time, Pallas kernels for 0%

commit v1 on v0

v1 whole, which is shorter than its diff:
```python
import functools
import math

import jax
import jax.numpy as jnp
import numpy as np
from jax import lax
from jax.experimental import pallas as pl
from jax.experimental.pallas import tpu as pltpu
from jax.sharding import PartitionSpec as P

MESH = pl.DeviceIdType.MESH
BF = jnp.bfloat16
F32 = jnp.float32


def dot(a, b):
    return lax.dot_general(a, b, (((1,), (0,)), ((), ())), preferred_element_type=F32)


def dot_nt(a, b):
    return lax.dot_general(a, b, (((1,), (1,)), ((), ())), preferred_element_type=F32)


def dot_tn(a, b):
    return lax.dot_general(a, b, (((0,), (0,)), ((), ())), preferred_element_type=F32)


def split_rows(x):
    high = x.astype(BF)
    low = (x - high.astype(F32)).astype(BF)
    return jnp.concatenate([high, low], 0)


def leaky_and_slope(z):
    u = 4.0 * z
    t = jnp.exp(-jnp.abs(u))
    one = 1.0 + t
    soft = jnp.maximum(u, 0.0) + jnp.log(one)
    r = 1.0 / one
    sig = jnp.where(u >= 0.0, r, t * r)
    return 0.3 * z + 0.175 * soft, 0.3 + 0.7 * sig


ORDER2 = np.concatenate([np.arange(0, 128, 2), np.arange(1, 128, 2)])
ORDER1 = np.concatenate([2 * ORDER2, 2 * ORDER2 + 1])


def constants():
    expand = np.zeros((128, 1152), np.float32)
    for a in range(3):
        for e in range(3):
            for c in range(4):
                for h in range(16):
                    col = a * 192 + e * 64 + c * 16 + h
                    row = lambda b: ((a * 3 + b) * 3 + e) * 4 + c
                    expand[row(1 + h % 2), col] = 1
                    if h % 2:
                        expand[row(0), 576 + col] = 1
    halo = np.zeros((128, 1024), np.float32)
    for i in range(4):
        for a in range(3):
            d = 2 * i - 1 + a
            s, plane = (0, d) if d >= 0 else (1, 7)
            for e in range(3):
                for c in range(4):
                    row = (a * 9 + e) * 4 + c
                    halo[row, i * 256 + e * 64 + s * 32 + plane * 4 + c] = 1
    columns = np.zeros((512, 768), np.float32)
    for e in range(3):
        for p in range(256):
            w = 2 * ORDER1[p] - 1 + e
            if w >= 0:
                columns[w, e * 256 + p] = 1
    where2 = {int(l): q for q, l in enumerate(ORDER2)}
    shift2 = np.zeros((128, 128), np.float32)
    for p in range(128):
        if ORDER2[p] >= 1:
            shift2[where2[int(ORDER2[p]) - 1], p] = 1
    taps3 = np.zeros((256, 384), np.float32)
    for jj in range(2):
        for e in range(3):
            for l in range(64):
                w = 2 * l - 1 + e
                if w >= 0:
                    taps3[jj * 128 + where2[w], e * 128 + jj * 64 + l] = 1
    last = np.zeros((32, 512), np.float32)
    for d in range(8):
        for c in range(4):
            last[d * 4 + c, c * 128 + d * 16 + 15] = 1
    return [jnp.asarray(x, BF) for x in (expand, halo, columns, shift2, taps3, last, np.eye(64))]


class Plan:
    def __init__(self, nd, nh):
        self.nd, self.nh = nd, nh
        self.pb = 128 // nh
        self.mb = 64 // nh
        self.w3 = max(128, 2048 // nd)
        self.w2 = max(128, 1024 // nd)
        self.nv3 = -(-1728 // self.w3)
        self.nv2 = -(-864 // self.w2)
        names = ["vd", "vh", "vc", "ad", "ah", "ac", "bd", "bh", "bc", "2d", "2h", "2c", "1d", "1h", "1c"]
        self.sem = {}
        count = 0
        for name in names:
            self.sem[name] = count
            count += 1
        for name in ["w3", "cot", "out", "g3h", "g2h", "g2z", "g1h"]:
            self.sem[name] = count
            count += nh - 1
        for name in ["g3d", "g3a", "g2d", "g2a", "g1d"]:
            self.sem[name] = count
            count += nd - 1
        self.count = count

    def scratch(self):
        nd, nh, pb, mb = self.nd, self.nh, self.pb, self.mb
        v = pltpu.VMEM
        return dict(
            V0=v((4, 16, 512), BF),
            HS=v((32, 512), BF),
            HR=v((2, 32, 512), BF),
            T1=v((9, 192, 256), BF),
            TH=v((192, 256), BF),
            WT=v((256, 576), BF),
            WH=v((4, 32, 192), BF),
            PH=v((4, 32, 256), F32),
            A1=v((5, 288, 256), BF),
            S1=v((4, 256, 256), F32),
            T2=v((5, 864, 128), BF),
            W2T=v((3, 64, 288), BF),
            A2=v((3, 320, 128), BF),
            S2=v((2, 256, 128), F32),
            T3=v((3, 576, 128), BF),
            W3=v((nh, pb, 1728), BF),
            COT=v((nh, pb, 128), BF),
            OS=v((nh, pb, 128), BF),
            OR=v((nh, pb, 128), BF),
            D3=v((1728, 128), F32),
            SD2=v((256, 128), BF),
            SH2=v((2, 64, 128), BF),
            SC2=v((64, 128), BF),
            RD2=v((256, 128), BF),
            RH2=v((2, 64, 128), BF),
            RC2=v((64, 128), BF),
            B2=v((2, 256, 128), F32),
            DL2=v((2, 256, 128), BF),
            SD1=v((256, 256), BF),
            SH1=v((4, 32, 256), BF),
            SC1=v((32, 256), BF),
            RD1=v((256, 256), BF),
            RH1=v((4, 32, 256), BF),
            RC1=v((32, 256), BF),
            Y=v((4, 288, 128), F32),
            B1=v((4, 256, 256), F32),
            DL1=v((4, 256, 256), BF),
            G3F=v((nh, pb, 1728), F32),
            G3S=v((nh, pb, 1728), BF),
            R3H=v((nh, pb, 1728), BF),
            P3S=v((nd, pb, self.w3), F32),
            R3D=v((nd, pb, self.w3), F32),
            F3=v((nd, pb, self.w3), F32),
            Q3=v((pb, self.w3), F32),
            G2S=v((nh, mb, 864), F32),
            R2H=v((nh, mb, 864), F32),
            P2S=v((nd, mb, self.w2), F32),
            R2D=v((nd, mb, self.w2), F32),
            F2=v((nd, mb, self.w2), F32),
            Q2=v((mb, self.w2), F32),
            F2H=v((nh, nd, mb, self.w2), F32),
            G1A=v((256, 576), F32),
            G1S=v((32, 128), F32),
            R1H=v((nh, 32, 128), F32),
            G1D=v((32, 128), F32),
            R1D=v((nd, 32, 128), F32),
            ss=pltpu.SemaphoreType.DMA((self.count,)),
            rs=pltpu.SemaphoreType.DMA((self.count,)),
        )


def kernel(plan, names, scales, *refs):
    nd, nh, pb, mb = plan.nd, plan.nh, plan.pb, plan.mb
    vol, w1n, w2, w3t, cot, expand, halo, columns, shift2, taps3, last, eye = refs[:12]
    o3, g1o, g2o, g3o = refs[12:16]
    s = dict(zip(names, refs[16:]))
    ss, rs = s["ss"], s["rs"]
    dev, ha = lax.axis_index("dev"), lax.axis_index("ha")
    up_d, up_h = dev < nd - 1, ha < nh - 1
    lo_d, lo_h = dev > 0, ha > 0
    up_c, lo_c = up_d & up_h, lo_d & lo_h

    def dev_peer(k):
        return lax.rem(dev + k, nd)

    def ha_peer(k):
        return lax.rem(ha + k, nh)

    if nd * nh > 1:
        barrier = pltpu.get_barrier_semaphore()
        for k in range(1, nh):
            pl.semaphore_signal(barrier, inc=1, device_id=(dev, ha_peer(k)), device_id_type=MESH)
        for k in range(1, nd):
            pl.semaphore_signal(barrier, inc=1, device_id=(dev_peer(k), ha), device_id_type=MESH)

        @pl.when(up_c)
        def _():
            pl.semaphore_signal(barrier, inc=1, device_id=(dev + 1, ha + 1), device_id_type=MESH)

        @pl.when(lo_c)
        def _():
            pl.semaphore_signal(barrier, inc=1, device_id=(dev - 1, ha - 1), device_id_type=MESH)

    def copy(src, dst, k, target):
        return pltpu.make_async_remote_copy(
            src_ref=src, dst_ref=dst, send_sem=ss.at[k], recv_sem=rs.at[k], device_id=target, device_id_type=MESH
        )

    routes = {
        "d": (up_d, lo_d, nd > 1, (jnp.minimum(dev + 1, nd - 1), ha)),
        "h": (up_h, lo_h, nh > 1, (dev, jnp.minimum(ha + 1, nh - 1))),
        "c": (up_c, lo_c, nd > 1 and nh > 1, (jnp.minimum(dev + 1, nd - 1), jnp.minimum(ha + 1, nh - 1))),
    }
    back = {
        "d": (lo_d, up_d, nd > 1, (jnp.maximum(dev - 1, 0), ha)),
        "h": (lo_h, up_h, nh > 1, (dev, jnp.maximum(ha - 1, 0))),
        "c": (lo_c, up_c, nd > 1 and nh > 1, (jnp.maximum(dev - 1, 0), jnp.maximum(ha - 1, 0))),
    }
    pending = []

    def send(group, kind, src, dst, table=routes):
        can_send, can_receive, exists, target = table[kind]
        if not exists:
            return
        c = copy(src, dst, plan.sem[group + kind], target)
        pl.when(can_send)(c.start)
        pending.append((can_send, c))

    def receive(group, kind, src, dst, table=routes):
        can_send, can_receive, exists, target = table[kind]
        if not exists:
            return
        c = copy(src, dst, plan.sem[group + kind], target)
        pl.when(can_receive)(c.wait_recv)

    def blank(kind, ref, table=routes):
        can_send, can_receive, exists, target = table[kind]

        @pl.when(jnp.logical_not(can_receive))
        def _():
            ref[...] = jnp.zeros(ref.shape, ref.dtype)

    v2 = vol[...].reshape(512, 512)
    s["HS"][...] = dot(last[...], v2).astype(BF)

    blank("d", s["V0"])
    blank("h", s["HR"].at[0])
    blank("c", s["HR"].at[1])
    blank("h", s["A1"].at[1:5, 0:32])
    blank("d", s["A1"].at[0, 32:288])
    blank("c", s["A1"].at[0, 0:32])
    blank("h", s["A2"].at[1:3, 0:64])
    blank("d", s["A2"].at[0, 64:320])
    blank("c", s["A2"].at[0, 0:64])
    for n in ("1", "2"):
        blank("d", s["RD" + n], back)
        blank("h", s["RH" + n], back)
        blank("c", s["RC" + n], back)

    if nd * nh > 1:
        count = nh - 1 + nd - 1 + up_c.astype(jnp.int32) + lo_c.astype(jnp.int32)
        pl.semaphore_wait(barrier, count)

    halos_v = [
        ("d", vol.at[:, 7], s["V0"]),
        ("h", s["HS"], s["HR"].at[0]),
        ("c", s["HS"], s["HR"].at[1]),
    ]
    for kind, src, dst in halos_v:
        send("v", kind, src, dst)

    def spread(group, src_of, dst, size, peer_of, valid_send=None, valid_receive=None):
        made = []
        for k in range(1, size):
            peer = peer_of(k)
            target = (dev, peer) if peer_of is ha_peer else (peer, ha)
            c = copy(src_of(peer), dst(k), plan.sem[group] + k - 1, target)
            if valid_send is None:
                c.start()
                pending.append((None, c))
            else:
                ok = valid_send(peer)
                pl.when(ok)(c.start)
                pending.append((ok, c))
            made.append((k, c))
        return made

    def gather(made, valid_receive=None, size=None, me=None):
        for k, c in made:
            if valid_receive is None:
                c.wait_recv()
            else:
                pl.when(valid_receive(lax.rem(me + size - k, size)))(c.wait_recv)

    made_w3 = spread("w3", lambda p: w3t, lambda k: s["W3"].at[ha], nh, ha_peer)
    made_cot = spread("cot", lambda p: cot.at[p], lambda k: s["COT"].at[ha], nh, ha_peer)
    s["W3"][ha] = w3t[...]
    s["COT"][ha] = cot[ha]

    def store_taps(block, plane, channel):
        taps = dot(block, columns[...]).astype(BF)
        for d in range(block.shape[0] // 16):
            for e in range(3):
                s["T1"][plane + d, pl.ds(e * 64 + channel * 16, 16), :] = taps[d * 16 : d * 16 + 16, e * 256 : e * 256 + 256]

    for c in range(4):
        store_taps(vol[c].reshape(128, 512), 1, c)

    base = dot(w1n[...], expand[...])
    base_a, base_b = base[:, 0:576], base[:, 576:1152]
    row_h = lax.broadcasted_iota(jnp.int32, (32, 576), 1) & 15

    def tap_masks(j):
        return (row_h >> 1) == j, ((row_h & 1) == 1) & (((row_h + 1) >> 1) == j)

    for j in range(8):
        mask_a, mask_b = tap_masks(j)
        s["WT"][pl.ds(j * 32, 32), :] = (jnp.where(mask_a, base_a, 0.0) + jnp.where(mask_b, base_b, 0.0)).astype(BF)
    edge = dot(w1n[...], halo[...]).astype(BF)
    for i in range(4):
        s["WH"][i] = edge[:, i * 256 : i * 256 + 192]
    for a in range(3):
        s["W2T"][a] = dot_nt(eye[...], w2[a * 288 : a * 288 + 288, :]).astype(BF)

    for kind, src, dst in halos_v:
        receive("v", kind, src, dst)
    for c in range(4):
        store_taps(s["V0"][c], 0, c)
    rows = dot(s["HR"][...].reshape(64, 512), columns[...]).astype(BF)
    for e in range(3):
        s["TH"][pl.ds(e * 64, 64), :] = rows[:, e * 256 : e * 256 + 256]
    s["PH"][...] = dot(s["WH"][...].reshape(128, 192), s["TH"][...]).reshape(4, 32, 256)

    def first(i):
        z = dot(s["WT"][...], s["T1"][pl.ds(2 * i, 3)].reshape(576, 256))
        z = jnp.concatenate([z[0:32] + s["PH"][i], z[32:256]], 0)
        act, slope = leaky_and_slope(z)
        s["A1"][i + 1, 32:288, :] = act.astype(BF)
        s["S1"][i] = slope

    def second_taps(plane, lo, hi):
        x = s["A1"][plane, lo * 32 : hi * 32, :]
        moved = dot(x[:, 128:256], shift2[...]).astype(BF)
        for j in range(lo, hi):
            r = (j - lo) * 32
            s["T2"][plane, pl.ds(j * 96, 32), :] = moved[r : r + 32]
            s["T2"][plane, pl.ds(j * 96 + 32, 32), :] = x[r : r + 32, 0:128]
            s["T2"][plane, pl.ds(j * 96 + 64, 32), :] = x[r : r + 32, 128:256]

    first(3)
    halos_a = [
        ("d", s["A1"].at[4, 32:288], s["A1"].at[0, 32:288]),
        ("c", s["A1"].at[4, 256:288], s["A1"].at[0, 0:32]),
        ("h", s["A1"].at[1:5, 256:288], s["A1"].at[1:5, 0:32]),
    ]
    send("a", *halos_a[0])
    send("a", *halos_a[1])

    def loop_first(i, carry):
        first(i)
        return carry

    lax.fori_loop(0, 3, loop_first, 0)
    send("a", *halos_a[2])

    def loop_taps(i, carry):
        second_taps(i, 1, 9)
        return carry

    lax.fori_loop(1, 5, loop_taps, 0)
    for halo_a in halos_a:
        receive("a", *halo_a)
    second_taps(0, 0, 9)
    for plane in range(1, 5):
        second_taps(plane, 0, 1)

    for i in (1, 0):
        for j in range(4):
            z = None
            for a in range(3):
                term = dot(s["W2T"][a], s["T2"][2 * i + a, j * 192 : j * 192 + 288, :])
                z = term if z is None else z + term
            act, slope = leaky_and_slope(z)
            s["A2"][i + 1, 64 + 64 * j : 128 + 64 * j, :] = act.astype(BF)
            s["S2"][i, 64 * j : 64 * j + 64, :] = slope
    halos_b = [
        ("d", s["A2"].at[2, 64:320], s["A2"].at[0, 64:320]),
        ("c", s["A2"].at[2, 256:320], s["A2"].at[0, 0:64]),
        ("h", s["A2"].at[1:3, 256:320], s["A2"].at[1:3, 0:64]),
    ]
    for halo_b in halos_b:
        send("b", *halo_b)

    def third_taps(plane, b):
        x = jnp.concatenate(
            [s["A2"][plane, b * 64 : b * 64 + 64, :], s["A2"][plane, b * 64 + 128 : b * 64 + 192, :]], 1
        )
        y = dot(x, taps3[...]).astype(BF)
        for e in range(3):
            s["T3"][plane, b * 192 + e * 64 : b * 192 + e * 64 + 64, :] = y[:, e * 128 : e * 128 + 128]

    for plane in (1, 2):
        for b in (1, 2):
            third_taps(plane, b)
    for halo_b in halos_b:
        receive("b", *halo_b)
    for plane, b in ((0, 0), (0, 1), (0, 2), (1, 0), (2, 0)):
        third_taps(plane, b)
    gather(made_w3)
    gather(made_cot)
    w3 = s["W3"][...].reshape(128, 1728)
    t3 = s["T3"][...].reshape(1728, 128)
    act, slope = leaky_and_slope(dot(w3, t3))
    s["OS"][...] = act.astype(BF).reshape(nh, pb, 128)
    delta3 = (s["COT"][...].reshape(128, 128).astype(F32) * slope).astype(BF)

    s["D3"][...] = dot_tn(w3, delta3)

    def third_back(a):
        parts = []
        for b in range(3):
            r = a * 576 + b * 192
            x = jnp.concatenate([s["D3"][r + 64 * e : r + 64 * e + 64, :] for e in range(3)], 1)
            y = dot_nt(split_rows(x), taps3[...])
            parts.append(y[0:64] + y[64:128])
        left = [y[:, 0:128] for y in parts]
        right = [y[:, 128:256] for y in parts]
        return [left[0], left[1], left[2] + right[0], right[1], right[2]]

    k = third_back(0)
    s["SC2"][...] = k[0].astype(BF)
    for j in range(4):
        s["SD2"][64 * j : 64 * j + 64, :] = k[j + 1].astype(BF)
    for i in range(2):
        k = third_back(i + 1)
        s["SH2"][i] = k[0].astype(BF)
        for j in range(4):
            s["B2"][i, 64 * j : 64 * j + 64, :] = k[j + 1]
    halos_2 = [("d", s["SD2"], s["RD2"]), ("c", s["SC2"], s["RC2"]), ("h", s["SH2"], s["RH2"])]
    for kind, src, dst in halos_2:
        send("2", kind, src, dst, back)
    made_out = spread("out", lambda p: s["OS"].at[p], lambda k: s["OR"].at[ha], nh, ha_peer)
    s["OR"][ha] = s["OS"][ha]
    g3 = dot_nt(delta3, t3)
    s["G3F"][...] = g3.reshape(nh, pb, 1728)
    s["G3S"][...] = g3.astype(BF).reshape(nh, pb, 1728)
    made_g3h = spread("g3h", lambda p: s["G3S"].at[p], lambda k: s["R3H"].at[k], nh, ha_peer)

    for kind, src, dst in halos_2:
        receive("2", kind, src, dst, back)
    s["B2"][1] += s["RD2"][...].astype(F32)
    s["B2"][1, 192:256, :] += s["RC2"][...].astype(F32)
    for i in range(2):
        s["B2"][i, 192:256, :] += s["RH2"][i].astype(F32)
    s["DL2"][...] = (s["B2"][...] * s["S2"][...]).astype(BF)

    lane = lax.broadcasted_iota(jnp.int32, (32, 128), 1)

    def second_back(pairs, store):
        for j in range(4):
            y = None
            for a, i in pairs:
                term = dot(w2[a * 288 : a * 288 + 288, :], s["DL2"][i, j * 64 : j * 64 + 64, :])
                y = term if y is None else y + term
            s["Y"][j] = y
        for k in range(9):
            if k % 2:
                d = s["Y"][k // 2, 96:192, :]
            else:
                d = None
                if k < 8:
                    d = s["Y"][k // 2, 0:96, :]
                if k > 0:
                    more = s["Y"][k // 2 - 1, 192:288, :]
                    d = more if d is None else d + more
            moved = jnp.where(lane < 64, pltpu.roll(d[0:32], 64, 1), pltpu.roll(d[0:32], 63, 1))
            moved = jnp.where(lane == 127, 0.0, moved)
            store(k, d[32:64], d[64:96] + moved)

    def store_plane0(k, even, odd):
        ref = s["SC1"] if k == 0 else s["SD1"].at[32 * k - 32 : 32 * k]
        ref[:, 0:128] = even.astype(BF)
        ref[:, 128:256] = odd.astype(BF)

    def store_plane(plane):
        def store(k, even, odd):
            if k == 0:
                s["SH1"][plane - 1, :, 0:128] = even.astype(BF)
                s["SH1"][plane - 1, :, 128:256] = odd.astype(BF)
            else:
                s["B1"][plane - 1, 32 * k - 32 : 32 * k, 0:128] = even
                s["B1"][plane - 1, 32 * k - 32 : 32 * k, 128:256] = odd

        return store

    halos_1 = [("d", s["SD1"], s["RD1"]), ("c", s["SC1"], s["RC1"]), ("h", s["SH1"], s["RH1"])]
    second_back([(0, 0)], store_plane0)
    send("1", *halos_1[0], back)
    send("1", *halos_1[1], back)
    second_back([(1, 0)], store_plane(1))
    second_back([(2, 0), (0, 1)], store_plane(2))
    second_back([(1, 1)], store_plane(3))
    second_back([(2, 1)], store_plane(4))
    send("1", *halos_1[2], back)

    g2 = None
    for i in range(2):
        for j in (0, 2):
            x = jnp.concatenate([s["DL2"][i, 64 * (j + t) : 64 * (j + t) + 64, :] for t in (0, 1)], 1)
            t2 = jnp.concatenate(
                [s["T2"][2 * i : 2 * i + 3, 192 * (j + t) : 192 * (j + t) + 288, :].reshape(864, 128) for t in (0, 1)], 1
            )
            term = dot_nt(x, t2)
            g2 = term if g2 is None else g2 + term
    s["G2S"][...] = g2.reshape(nh, mb, 864)
    made_g2h = spread("g2h", lambda p: s["G2S"].at[p], lambda k: s["R2H"].at[k], nh, ha_peer)

    def pieces(total, dst, width, size, valid):
        for r in range(valid):
            end = min(size, (r + 1) * width)
            if end < (r + 1) * width:
                dst[r] = jnp.zeros(dst.shape[1:], F32)
            dst[r, :, 0 : end - r * width] = total[:, r * width : end]

    gather(made_g3h)
    total = s["G3F"][ha]
    for k in range(1, nh):
        total = total + s["R3H"][k].astype(F32)
    pieces(total, s["P3S"], plan.w3, 1728, plan.nv3)
    made_g3d = spread(
        "g3d", lambda p: s["P3S"].at[p], lambda k: s["R3D"].at[k], nd, dev_peer, lambda p: p < plan.nv3
    )

    for kind, src, dst in halos_1:
        receive("1", kind, src, dst, back)
    s["B1"][3] += s["RD1"][...].astype(F32)
    s["B1"][3, 224:256, :] += s["RC1"][...].astype(F32)
    for i in range(4):
        s["B1"][i, 224:256, :] += s["RH1"][i].astype(F32)
    s["G1A"][...] = jnp.zeros((256, 576), F32)

    def loop_back(i, carry):
        d = (s["B1"][i] * s["S1"][i]).astype(BF)
        s["DL1"][i] = d
        s["G1A"][...] += dot_nt(d, s["T1"][pl.ds(2 * i, 3)].reshape(576, 256))
        return carry

    lax.fori_loop(0, 4, loop_back, 0)
    gh = dot_nt(s["DL1"][:, 0:32, :].reshape(128, 256), s["TH"][...])
    sum_a = jnp.zeros((32, 576), F32)
    sum_b = jnp.zeros((32, 576), F32)
    for j in range(8):
        mask_a, mask_b = tap_masks(j)
        g = s["G1A"][32 * j : 32 * j + 32, :]
        sum_a = sum_a + jnp.where(mask_a, g, 0.0)
        sum_b = sum_b + jnp.where(mask_b, g, 0.0)
    g1 = dot_nt(split_rows(sum_a), expand[:, 0:576])
    g1 = g1 + dot_nt(split_rows(sum_b), expand[:, 576:1152])
    for i in range(4):
        g1 = g1 + dot_nt(split_rows(gh[32 * i : 32 * i + 32]), halo[:, i * 256 : i * 256 + 192])
    s["G1S"][...] = g1[0:32] + g1[32:64]
    made_g1h = spread("g1h", lambda p: s["G1S"], lambda k: s["R1H"].at[k], nh, ha_peer)

    gather(made_g2h)
    total = s["G2S"][ha]
    for k in range(1, nh):
        total = total + s["R2H"][k]
    pieces(total, s["P2S"], plan.w2, 864, plan.nv2)
    made_g2d = spread(
        "g2d", lambda p: s["P2S"].at[p], lambda k: s["R2D"].at[k], nd, dev_peer, lambda p: p < plan.nv2
    )

    def sum_pieces(made, own, received, dst, flat, group, valid):
        mine = dev < valid

        @pl.when(mine)
        def _():
            total = own[dev]
            for k, c in made:
                c.wait_recv()
                total = total + received[k]
            flat[...] = total
            dst[dev] = total

        return spread(group, lambda p: flat, lambda k: dst.at[dev], nd, dev_peer, lambda p: mine)

    made_g3a = sum_pieces(made_g3d, s["P3S"], s["R3D"], s["F3"], s["Q3"], "g3a", plan.nv3)

    gather(made_g1h)
    total = s["G1S"][...]
    for k in range(1, nh):
        total = total + s["R1H"][k]
    s["G1D"][...] = total
    made_g1d = spread("g1d", lambda p: s["G1D"], lambda k: s["R1D"].at[k], nd, dev_peer)

    made_g2a = sum_pieces(made_g2d, s["P2S"], s["R2D"], s["F2"], s["Q2"], "g2a", plan.nv2)

    gather(made_g2a, lambda src: src < plan.nv2, nd, dev)
    made_g2z = spread(
        "g2z", lambda p: s["F2"].at[0 : plan.nv2], lambda k: s["F2H"].at[ha, 0 : plan.nv2], nh, ha_peer
    )
    s["F2H"][ha, 0 : plan.nv2] = s["F2"][0 : plan.nv2]

    gather(made_g1d)
    total = s["G1D"][...]
    for k in range(1, nd):
        total = total + s["R1D"][k]
    g1o[...] = total * scales[0]
    gather(made_g3a, lambda src: src < plan.nv3, nd, dev)
    g3o[...] = s["F3"][0 : plan.nv3] * scales[2]
    gather(made_out)
    o3[...] = s["OR"][...]
    gather(made_g2z)
    g2o[...] = s["F2H"][:, 0 : plan.nv2] * scales[1]

    for ok, c in pending:
        if ok is None:
            c.wait_send()
        else:
            pl.when(ok)(c.wait_send)


def local(nd, nh, volume, w_first, w_second, w_third, cotangent):
    plan = Plan(nd, nh)
    pb, mb = plan.pb, plan.mb
    cells = volume.shape[1] * nd * volume.shape[2] * nh * volume.shape[3]
    scales = tuple(1.0 / math.sqrt(cells // 8 ** n) for n in (1, 2, 3))
    w1n = jnp.pad(w_first.reshape(108, 32).T, ((0, 0), (0, 20)))
    w2 = w_second.reshape(864, 64)
    w3t = w_third.reshape(1728, pb).T
    cot = jnp.transpose(cotangent.reshape(pb, nh, 128), (1, 0, 2))
    scratch = plan.scratch()
    names = list(scratch)
    vmem = pl.BlockSpec(memory_space=pltpu.VMEM)
    out3, g1, g2, g3 = pl.pallas_call(
        functools.partial(kernel, plan, names, scales),
        out_shape=(
            jax.ShapeDtypeStruct((nh, pb, 128), BF),
            jax.ShapeDtypeStruct((32, 128), F32),
            jax.ShapeDtypeStruct((nh, plan.nv2, mb, plan.w2), F32),
            jax.ShapeDtypeStruct((plan.nv3, pb, plan.w3), F32),
        ),
        in_specs=[vmem] * 12,
        out_specs=(vmem,) * 4,
        scratch_shapes=[scratch[n] for n in names],
        compiler_params=pltpu.CompilerParams(
            collective_id=0 if nd * nh > 1 else None, has_side_effects=True, vmem_limit_bytes=60 * 2**20
        ),
        name="step",
    )(volume, w1n, w2, w3t, cot, *constants())
    out3 = jnp.transpose(out3.reshape(nh, pb, 2, 64), (1, 0, 2, 3)).reshape(pb, 1, 2 * nh, 64)
    g1 = g1[:, 0:108].T.reshape(3, 3, 3, 4, 32)
    g2 = jnp.transpose(g2, (1, 3, 0, 2)).reshape(plan.nv2 * plan.w2, 64)[0:864].reshape(3, 3, 3, 32, 64)
    g3 = jnp.transpose(g3, (0, 2, 1)).reshape(plan.nv3 * plan.w3, pb)[0:1728].reshape(3, 3, 3, 64, pb)
    return out3, g1, g2, g3


def solution(mesh):
    placed = (
        P(None, "dev", "ha", None),
        P(),
        P(),
        P(None, None, None, None, "ha"),
        P("ha", "dev", None, None),
    )
    return jax.shard_map(
        functools.partial(local, mesh.shape["dev"], mesh.shape["ha"]),
        mesh=mesh,
        in_specs=placed,
        out_specs=(P("ha", "dev", None, None), P(), P(), P(None, None, None, None, "ha")),
        check_vma=False,
    )
```

time: 810 us -> 68.5 us (0.08); the launches traced: 801 us -> 68.1 us
  waiting for transfers between devices: 291 us -> 0 us
  local copies, waits for them, and re-layouts: 210 us -> 7.94 us
  matrix products: 168 us -> 0 us
  blocking collectives: 63.8 us -> 0 us
  Pallas kernels: 0 us -> 59.5 us
  starting transfers between devices: 34.9 us -> 0 us
  other arithmetic: 18 us -> 0 us
  between operations: 14.9 us -> 0.69 us
    psum x2 -> x0, waiting for transfers between devices: 235 us -> none  [the longest x1 147 us: local(): lax.psum((local_first, local_second), ('dev', 'ha'))]
    transpose x3 -> x0, matrix products: 118 us -> none  [weight_grad(): return jnp.transpose(result, (2, 3, 4, 0, 1))]
    broadcast_in_dim x10 -> x0, local copies, waits for them, and re-layouts: 85.8 us -> none  [the longest x3 75.3 us: weight_grad(): inputs[:, None]]
    conv_general_dilated x17 -> x0, local copies, waits for them, and re-layouts: 71.2 us -> none  [the longest x9 43.6 us: convolve(): lax.conv_general_dilated(inputs[None], kernel, (2, 2, 2), [pad_depth, pad...]
    psum x1 -> x0, blocking collectives: 63.8 us -> none  [local(): lax.psum((local_first, local_second), ('dev', 'ha'))]
    pallas_call x0 -> x1, Pallas kernels: none -> 59.5 us  [local(): pl.pallas_call(functools.partial(kernel, plan, names, scales), out_shape=...]
    conv_general_dilated x5 -> x0, matrix products: 50.4 us -> none  [the longest x3 38.7 us: convolve(): lax.conv_general_dilated(inputs[None], kernel, (2, 2, 2), [pad_depth, pad...]
    all_gather x1 -> x0, waiting for transfers between devices: 48 us -> none  [local(): all_rows = lax.all_gather(deeper, 'ha', axis=2, tiled=True)]
  transfers between devices with their start and end apart: 12 -> 0, of which waited for: 8 -> 0; matrix products, arithmetic and copies ran while one was open for 17% -> 0% of each run, Pallas kernels for 0% -> 0%
where the time goes in v1:
time: 68.5 us; the launch traced here: 68.1 us
  Pallas kernels  59.5 us (87%)
  local copies, waits for them, and re-layouts  7.94 us (12%)
  between operations  0.69 us (1%)
    pallas_call x1, Pallas kernels, local(): pl.pallas_call(functools.partial(kernel, plan, names, scales), out_shape=...  59.5 us
    unnamed x12, local copies, waits for them, and re-layouts  2.18 us

profile of v1, /device:TPU:1, one launch (start us, length us, event | category | flops | bytes accessed | tf_op | source)
XLA Modules:
  0.0 68.1 jit_solution(12365602419634563211)
XLA Ops:
  0.6 1.0 %copy.29 = bf16[3,3,3,64,16]{3,2,1,0,4:T(4,128)(2,1)S(1)} copy(bf16[3,3,3,64,16]{3,4,2,1,0:T(8,128)(2,1)} %param.15) | data formatting | bytes 110592 | tf_op args[3]
  1.6 0.0 copy-start.1
  1.6 0.8 %reshape.43 = bf16[1728,16]{0,1:T(8,128)(2,1)} reshape(bf16[3,3,3,64,16]{3,2,1,0,4:T(4,128)(2,1)S(1)} %copy.29) | data formatting | bytes 110592 | tf_op jit(solution)/shard_map/reshape | solution.py:640
  2.4 0.1 copy-done.1
  2.4 0.1 reshape.44
  2.5 0.0 copy-start.3
  2.5 0.6 copy.39
  3.2 0.1 copy-done.3
  3.3 0.1 copy.28
  3.4 0.6 pad.4.refs_1_
  4.0 59.5 %step.1 = (bf16[8,16,128]{2,1,0:T(8,128)(2,1)}, f32[32,128]{1,0:T(8,128)}, f32[8,7,8,128]{3,2,1,0:T(8,128)}, f32[14,16,128]{2,1,0:T(8,128)}) custom-call(bf16[4,8,16,512]{3,2,1,0:T(8,128)(2,1)} %refs_0_.1, bf16[32,128]{1,0:T(8,128)(2,1)} %pad.4.refs_1_, bf16[864,64]{1,0:T(8,128)(2,1)} %bitcast.33, bf16[16,1728]{1,0:T(8,128)(2,1)} %bitcast.31, ...), custom_call_target="tpu_custom_call" | custom-call | tf_op jit(solution)/shard_map/step/pallas_call | solution.py:645
  63.5 0.9 %copy_bitcast_fusion = f32[1792,16]{0,1:T(8,128)S(1)} fusion(f32[14,16,128]{2,1,0:T(8,128)} %get-tuple-element.11), kind=kLoop, calls=%fused_computation | loop fusion | bytes 229376 | tf_op jit(solution)/shard_map/reshape | solution.py:664
  64.4 0.2 reshape.51
  64.6 0.0 copy-start
  64.6 0.7 %copy.35 = f32[3,3,3,64,16]{3,4,2,1,0:T(8,128)} copy(f32[3,3,3,64,16]{3,2,1,0,4:T(4,128)S(1)} %reshape.51) | data formatting | bytes 221184
  65.3 0.3 copy-done
  65.6 0.0 copy-start.2
  65.6 1.0 %copy.33 = f32[864,64]{1,0:T(8,128)} copy(f32[864,64]{0,1:T(8,128)S(1)} %bitcast.32) | data formatting | bytes 442368 | tf_op jit(solution)/shard_map/slice | solution.py:663
  66.5 0.0 copy-done.2
  66.6 0.1 reshape.45
  66.6 0.0 copy-start.4
  66.7 0.7 copy.31
  67.3 0.0 copy-done.4
  67.4 0.1 copy.32
  67.5 0.6 reshape.47
  (2 shorter events, 0.0 us)
Async XLA Ops:
  1.6 0.8 %copy-start.1 = (bf16[16,1,16,64]{3,2,1,0:T(8,128)(2,1)S(1)}, bf16[16,1,16,64]{3,2,1,0:T(8,128)(2,1)}, u32[]{:S(2)}) copy-start(bf16[16,1,16,64]{3,2,1,0:T(8,128)(2,1)} %param.16) | copy-start | bytes 98308
  2.5 0.7 %copy-start.3 = (bf16[3,3,3,4,32]{4,3,2,1,0:T(4,128)(2,1)S(1)}, bf16[3,3,3,4,32]{4,3,2,1,0:T(4,128)(2,1)}, u32[]{:S(2)}) copy-start(bf16[3,3,3,4,32]{4,3,2,1,0:T(4,128)(2,1)} %param.13) | copy-start | bytes 20740
  64.6 1.0 %copy-start = (f32[8,7,8,128]{3,2,1,0:T(8,128)S(1)}, f32[8,7,8,128]{3,2,1,0:T(8,128)}, u32[]{:S(2)}) copy-start(f32[8,7,8,128]{3,2,1,0:T(8,128)} %get-tuple-element.10) | copy-start | bytes 688132
  65.6 1.0 %copy-start.2 = (bf16[8,16,128]{2,1,0:T(8,128)(2,1)S(1)}, bf16[8,16,128]{2,1,0:T(8,128)(2,1)}, u32[]{:S(2)}) copy-start(bf16[8,16,128]{2,1,0:T(8,128)(2,1)} %get-tuple-element.8) | copy-start | bytes 98308
  66.6 0.7 %copy-start.4 = (f32[32,128]{1,0:T(8,128)S(1)}, f32[32,128]{1,0:T(8,128)}, u32[]{:S(2)}) copy-start(f32[32,128]{1,0:T(8,128)} %get-tuple-element.9) | copy-start | bytes 49156

commit v2 on v0

v2 whole, which is shorter than its diff:
```python
import functools
import math
import types

import jax
import jax.numpy as jnp
import numpy as np
from jax import lax
from jax.experimental import pallas as pl
from jax.experimental.pallas import tpu as pltpu
from jax.sharding import PartitionSpec as P

MESH = pl.DeviceIdType.MESH
BF = jnp.bfloat16
F32 = jnp.float32


def dot(a, b):
    return lax.dot_general(a, b, (((1,), (0,)), ((), ())), preferred_element_type=F32)


def dot_nt(a, b):
    return lax.dot_general(a, b, (((1,), (1,)), ((), ())), preferred_element_type=F32)


def dot_tn(a, b):
    return lax.dot_general(a, b, (((0,), (0,)), ((), ())), preferred_element_type=F32)


def split_rows(x):
    high = x.astype(BF)
    low = (x - high.astype(F32)).astype(BF)
    return jnp.concatenate([high, low], 0)


def leaky_and_slope(z):
    soft = jnp.log(1.0 + jnp.exp(-4.0 * jnp.abs(z)))
    act = jnp.maximum(z, 0.3 * z) + 0.175 * soft
    return act, 0.65 + 0.35 * jnp.tanh(2.0 * z)


ORDER2 = np.concatenate([np.arange(0, 128, 2), np.arange(1, 128, 2)])
ORDER1 = np.concatenate([2 * ORDER2, 2 * ORDER2 + 1])


def constants(nh):
    expand = np.zeros((128, 1152), np.float32)
    for a in range(3):
        for e in range(3):
            for c in range(4):
                for h in range(16):
                    col = a * 192 + e * 64 + c * 16 + h
                    row = lambda b: ((a * 3 + b) * 3 + e) * 4 + c
                    expand[row(1 + h % 2), col] = 1
                    if h % 2:
                        expand[row(0), 576 + col] = 1
    halo = np.zeros((128, 1024), np.float32)
    for i in range(4):
        for a in range(3):
            d = 2 * i - 1 + a
            s, plane = (0, d) if d >= 0 else (1, 7)
            for e in range(3):
                for c in range(4):
                    row = (a * 9 + e) * 4 + c
                    halo[row, i * 256 + e * 64 + s * 32 + plane * 4 + c] = 1
    columns = np.zeros((512, 768), np.float32)
    for e in range(3):
        for p in range(256):
            w = 2 * ORDER1[p] - 1 + e
            if w >= 0:
                columns[w, e * 256 + p] = 1
    where2 = {int(l): q for q, l in enumerate(ORDER2)}
    shift2 = np.zeros((128, 128), np.float32)
    for p in range(128):
        if ORDER2[p] >= 1:
            shift2[where2[int(ORDER2[p]) - 1], p] = 1
    taps3 = np.zeros((256, 384), np.float32)
    for jj in range(2):
        for e in range(3):
            for l in range(64):
                w = 2 * l - 1 + e
                if w >= 0:
                    taps3[jj * 128 + where2[w], e * 128 + jj * 64 + l] = 1
    last = np.zeros((32, 512), np.float32)
    for d in range(8):
        for c in range(4):
            last[d * 4 + c, c * 128 + d * 16 + 15] = 1
    pb = 128 // nh
    rows = np.zeros((256, 256), np.float32)
    for jj in range(2):
        for q in range(nh):
            for ch in range(pb):
                rows[(jj * nh + q) * pb + ch, ch * 2 * nh + 2 * q + jj] = 1
    made = (expand, halo, columns, shift2, taps3, last, np.eye(64), rows)
    return [jnp.asarray(x, BF) for x in made]


class Plan:
    def __init__(self, nd, nh):
        self.nd, self.nh = nd, nh
        self.nc = 2 if nd > 1 else 1
        self.nz = nd // self.nc
        self.pb = 128 // nh
        self.mb = 64 // nh
        self.r2 = 512 // (self.nc * nh)
        self.half = 1792 // self.nc
        self.sem = {}
        count = 0
        names = ["vd0", "vd1", "vd2", "vd3", "vh", "vc", "adi", "adj", "ahi", "ahj", "ac", "bd", "bh", "bc", "3d", "3h", "3c", "sd", "sh", "sc"]
        for name in names + ["w3c", "g3c", "g3p"]:
            self.sem[name] = count
            count += 1
        for name in ["w3", "cot", "out", "g3h"]:
            self.sem[name] = count
            count += nh - 1
        for name in ["g2h", "g2z", "g1h"]:
            self.sem[name] = count
            count += nh * self.nc - 1
        for name in ["g3d", "g2d", "g1d"]:
            self.sem[name] = count
            count += self.nz - 1
        self.count = count

    def scratch(self):
        nd, nh, nc, pb, mb = self.nd, self.nh, self.nc, self.pb, self.mb
        v = pltpu.VMEM
        return dict(
            V0=v((64, 512), BF),
            HS=v((32, 512), BF),
            HR=v((2, 32, 512), BF),
            T1=v((9, 192, 256), BF),
            TH=v((192, 256), BF),
            W1F=v((128, 32), F32),
            WT=v((256, 576), BF),
            WH=v((4, 32, 192), BF),
            PH=v((4, 32, 256), F32),
            Z0=v((4, 32, 256), F32),
            A1=v((5, 288, 256), BF),
            S1=v((4, 256, 256), F32),
            T2=v((5, 864, 128), BF),
            W2T=v((3, 64, 288), BF),
            A2=v((3, 320, 128), BF),
            S2=v((2, 256, 128), F32),
            T3=v((3, 576, 128), BF),
            W3A=v((pb, 1792), BF),
            W3=v((nh, pb, 1792), BF),
            W3T=v((1792, 128), BF),
            CS=v((nh, pb, 128), BF),
            COT=v((nh, pb, 128), BF),
            OS=v((nh, pb, 128), BF),
            OR=v((nh, pb, 128), BF),
            D3=v((128, 128), BF),
            D3D=v((128, 128), BF),
            D3P=v((64, 128), BF),
            D3H=v((64, 128), BF),
            D3C=v((64, 128), BF),
            SS=v((2, 256, 128), BF),
            SD=v((256, 128), BF),
            SH=v((2, 64, 128), BF),
            SC=v((64, 128), BF),
            B2=v((3, 320, 128), F32),
            DL2=v((3, 320, 128), BF),
            Y=v((5, 288, 128), F32),
            B1=v((4, 256, 256), F32),
            DL1=v((4, 256, 256), BF),
            G3F=v((nh, pb, 1792), F32),
            G3S=v((nh, pb, 1792), BF),
            R3C=v((nh, pb, self.half), BF),
            G3T=v((nh, pb, self.half), F32),
            G3U=v((nh, pb, self.half), BF),
            R3H=v((nh, pb, self.half), BF),
            P3S=v((pb, self.half), BF),
            R3D=v((self.nz, pb, self.half), BF),
            P3F=v((pb, self.half), F32),
            F3=v((nc, pb, self.half), F32),
            G2F=v((nc, nh, self.r2, 128), F32),
            G2S=v((nc, nh, self.r2, 128), BF),
            R2H=v((nc * nh, self.r2, 128), BF),
            G2D=v((self.r2, 128), BF),
            R2D=v((self.nz, self.r2, 128), BF),
            F2=v((self.r2, 128), BF),
            F2H=v((nc, nh, self.r2, 128), BF),
            G1A=v((256, 576), F32),
            G1S=v((32, 128), BF),
            R1H=v((nc * nh, 32, 128), BF),
            G1D=v((32, 128), BF),
            R1D=v((self.nz, 32, 128), BF),
            G1O=v((32, 128), F32),
            ss=pltpu.SemaphoreType.DMA((self.count,)),
            rs=pltpu.SemaphoreType.DMA((self.count,)),
            ls=pltpu.SemaphoreType.DMA((16,)),
        )


INPUTS = ["vol", "w1", "w2", "w3", "cot", "expand", "halo", "columns", "shift2", "taps3", "last", "eye", "rows"]


def kernel(plan, names, *refs):
    nd, nh, nc, nz, pb, mb, half = plan.nd, plan.nh, plan.nc, plan.nz, plan.pb, plan.mb, plan.half
    inputs = dict(zip(INPUTS, refs[: len(INPUTS)]))
    o3, g1o, g2o, g3o = refs[len(INPUTS) : len(INPUTS) + 4]
    s = types.SimpleNamespace(**dict(zip(names, refs[len(INPUTS) + 4 :])))
    ss, rs = s.ss, s.rs
    dev, ha = lax.axis_index("dev"), lax.axis_index("ha")
    core, zy = (dev & 1, dev >> 1) if nc == 2 else (dev * 0, dev)
    up_d, up_h = dev < nd - 1, ha < nh - 1
    lo_d, lo_h = dev > 0, ha > 0
    up_c, lo_c = up_d & up_h, lo_d & lo_h

    order = ["vol", "w3", "last", "columns", "w1", "expand", "halo", "cot", "rows", "w2", "eye", "shift2", "taps3"]
    copies = {}
    for k, name in enumerate(order):
        copies[name] = pltpu.make_async_copy(inputs[name], getattr(s, "i_" + name), s.ls.at[k])
        copies[name].start()
    arrived = set()

    def take(name):
        if name not in arrived:
            arrived.add(name)
            copies[name].wait()
        return getattr(s, "i_" + name)

    sizes = {"h": nh, "a": nh * nc, "z": nz}

    def wrap(x, n):
        return x & (n - 1) if n & (n - 1) == 0 else lax.rem(x, n)

    peers = {"h": [(dev, wrap(ha + k, nh)) for k in range(nh)]}
    peers["z"] = [(wrap(zy + k, nz) * nc + core, ha) for k in range(nz)]
    peers["a"] = []
    for k in range(nh * nc):
        index = wrap(ha * nc + core + k, nh * nc)
        peers["a"].append((zy * nc + wrap(index, nc), index // nc if nc == 1 else index >> 1))

    def peer_of(group, k):
        return peers[group][k]

    if nd * nh > 1:
        barrier = pltpu.get_barrier_semaphore()
        count = 0
        for group in ("a", "z"):
            for k in range(1, sizes[group]):
                pl.semaphore_signal(barrier, inc=1, device_id=peer_of(group, k), device_id_type=MESH)
                count += 1
        last_core, first_core = core == nc - 1, core == 0
        for ok, target in (
            (up_d & last_core, (dev + 1, ha)),
            (lo_d & first_core, (dev - 1, ha)),
            (up_c & last_core, (dev + 1, ha + 1)),
            (lo_c & first_core, (dev - 1, ha - 1)),
        ):

            @pl.when(ok)
            def _():
                pl.semaphore_signal(barrier, inc=1, device_id=target, device_id_type=MESH)

            count = count + ok.astype(jnp.int32)

    def copy(src, dst, k, target):
        return pltpu.make_async_remote_copy(
            src_ref=src, dst_ref=dst, send_sem=ss.at[k], recv_sem=rs.at[k], device_id=target, device_id_type=MESH
        )

    routes = {
        "d": (up_d, lo_d, nd > 1, (jnp.minimum(dev + 1, nd - 1), ha)),
        "h": (up_h, lo_h, nh > 1, (dev, jnp.minimum(ha + 1, nh - 1))),
        "c": (up_c, lo_c, nd > 1 and nh > 1, (jnp.minimum(dev + 1, nd - 1), jnp.minimum(ha + 1, nh - 1))),
    }
    back = {
        "d": (lo_d, up_d, nd > 1, (jnp.maximum(dev - 1, 0), ha)),
        "h": (lo_h, up_h, nh > 1, (dev, jnp.maximum(ha - 1, 0))),
        "c": (lo_c, up_c, nd > 1 and nh > 1, (jnp.maximum(dev - 1, 0), jnp.maximum(ha - 1, 0))),
    }
    pending = []

    def send(name, src, dst, table=routes):
        can_send, can_receive, exists, target = table[name[1]]
        if not exists:
            return
        c = copy(src, dst, plan.sem[name], target)
        pl.when(can_send)(c.start)
        pending.append((can_send, c))

    def receive(name, src, dst, table=routes):
        can_send, can_receive, exists, target = table[name[1]]
        if not exists:
            return
        c = copy(src, dst, plan.sem[name], target)
        pl.when(can_receive)(c.wait_recv)

    def blank(kind, ref, table=routes):
        can_send, can_receive, exists, target = table[kind]

        @pl.when(jnp.logical_not(can_receive))
        def _():
            ref[...] = jnp.zeros(ref.shape, ref.dtype)

    def spread(group, name, src_of, dst, valid_send=None):
        made = []
        for k in range(1, sizes[group]):
            target = peer_of(group, k)
            c = copy(src_of(*target), dst(k), plan.sem[name] + k - 1, target)
            ok = None if valid_send is None else valid_send(target[0])
            if ok is None:
                c.start()
            else:
                pl.when(ok)(c.start)
            pending.append((ok, c))
            made.append((k, c))
        return made

    def gather(made, valid_receive=None):
        for k, c in made:
            if valid_receive is None:
                c.wait_recv()
            else:
                pl.when(valid_receive(lax.rem(zy + nz - k, nz)))(c.wait_recv)

    def to_partner(name, src, dst):
        c = copy(src, dst, plan.sem[name], (dev + 1 - 2 * core, ha))
        c.start()
        pending.append((None, c))
        return c

    blank("d", s.V0)
    blank("h", s.HR.at[0])
    s.HR[1, 0:16, :] = jnp.zeros((16, 512), BF)
    blank("c", s.HR.at[1, 16:32])
    blank("h", s.A1.at[1:5, 0:32])
    blank("d", s.A1.at[0, 32:288])
    blank("c", s.A1.at[0, 0:32])
    blank("h", s.A2.at[1:3, 0:64])
    blank("d", s.A2.at[0, 64:320])
    blank("c", s.A2.at[0, 0:64])
    blank("d", s.D3D, back)
    blank("h", s.D3H, back)
    blank("c", s.D3C, back)
    blank("d", s.SD, back)
    blank("h", s.SH, back)
    blank("c", s.SC, back)

    if nd * nh > 1:
        pl.semaphore_wait(barrier, count)
    halos_v = [("vd%d" % c, inputs["vol"].at[c, 7], s.V0.at[c * 16 : c * 16 + 16]) for c in range(4)]
    for halo_v in halos_v:
        send(*halo_v)
    w3_in = take("w3")
    for t in range(27):
        s.W3A[:, t * 64 : t * 64 + 64] = w3_in[t]
    s.W3A[:, 1728:1792] = jnp.zeros((pb, 64), BF)
    for c in range(nc):

        @pl.when(core == c)
        def _():
            s.W3[ha, :, c * half : c * half + half] = s.W3A[:, c * half : c * half + half]

    vol = take("vol")
    s.HS[...] = dot(take("last")[...], vol[...].reshape(512, 512)).astype(BF)
    halos_v = halos_v + [("vh", s.HS, s.HR.at[0]), ("vc", s.HS.at[16:32], s.HR.at[1, 16:32])]
    for halo_v in halos_v[4:]:
        send(*halo_v)

    def taps_of(rows):
        return dot(rows, take("columns")[...]).astype(BF)

    for c in range(4):
        taps = taps_of(vol[c].reshape(128, 512))
        for d in range(8):
            for e in range(3):
                s.T1[1 + d, e * 64 + c * 16 : e * 64 + c * 16 + 16, :] = taps[
                    d * 16 : d * 16 + 16, e * 256 : e * 256 + 256
                ]

    w1 = take("w1")
    s.W1F[96:128, :] = jnp.zeros((32, 32), F32)
    for t in range(27):
        s.W1F[4 * t : 4 * t + 4, :] = w1[t].astype(F32)
    w1b = s.W1F[...].astype(BF)
    base = dot_tn(w1b, take("expand")[...])
    base_a, base_b = base[:, 0:576], base[:, 576:1152]
    row_h = lax.broadcasted_iota(jnp.int32, (32, 576), 1) & 15

    def tap_masks(j):
        return (row_h >> 1) == j, ((row_h & 1) == 1) & (((row_h + 1) >> 1) == j)

    for j in range(8):
        mask_a, mask_b = tap_masks(j)
        s.WT[j * 32 : j * 32 + 32, :] = jnp.where(mask_a, base_a, jnp.where(mask_b, base_b, 0.0)).astype(BF)
    edge = dot_tn(w1b, take("halo")[...]).astype(BF)
    for i in range(4):
        s.WH[i] = edge[:, i * 256 : i * 256 + 192]

    def first(i):
        z = dot(s.WT[...], s.T1[pl.ds(2 * i, 3)].reshape(576, 256))
        s.Z0[i] = z[0:32]
        act, slope = leaky_and_slope(z[32:256])
        s.A1[i + 1, 64:288, :] = act.astype(BF)
        s.S1[i, 32:256, :] = slope

    def second_taps(plane, lo, hi):
        x = s.A1[plane, lo * 32 : hi * 32, :]
        moved = dot(x[:, 128:256], take("shift2")[...]).astype(BF)
        for j in range(lo, hi):
            r = (j - lo) * 32
            s.T2[plane, j * 96 : j * 96 + 32, :] = moved[r : r + 32]
            s.T2[plane, j * 96 + 32 : j * 96 + 64, :] = x[r : r + 32, 0:128]
            s.T2[plane, j * 96 + 64 : j * 96 + 96, :] = x[r : r + 32, 128:256]

    first(3)
    a1 = s.A1
    halo_adi = ("adi", a1.at[4, 64:288], a1.at[0, 64:288])
    halo_adj = ("adj", a1.at[4, 32:64], a1.at[0, 32:64])
    halo_ac = ("ac", a1.at[4, 256:288], a1.at[0, 0:32])
    halo_ahi = ("ahi", a1.at[2:5, 256:288], a1.at[2:5, 0:32])
    halo_ahj = ("ahj", a1.at[1, 256:288], a1.at[1, 0:32])
    send(*halo_adi)
    send(*halo_ac)

    def loop_first(i, carry):
        first(i)
        return carry

    lax.fori_loop(1, 3, loop_first, 0)
    send(*halo_ahi)

    my_half = pl.ds(pl.multiple_of(core * half, 128), half)
    made_w3 = spread("h", "w3", lambda d, h: s.W3A.at[:, my_half], lambda k: s.W3.at[ha, :, my_half])
    for halo_v in halos_v:
        receive(*halo_v)
    edges = taps_of(jnp.concatenate([s.V0[...], s.HR[...].reshape(64, 512)], 0))
    for e in range(3):
        s.T1[0, e * 64 : e * 64 + 64, :] = edges[0:64, e * 256 : e * 256 + 256]
        s.TH[e * 64 : e * 64 + 64, :] = edges[64:128, e * 256 : e * 256 + 256]
    s.PH[...] = dot(s.WH[...].reshape(128, 192), s.TH[...]).reshape(4, 32, 256)

    def top_rows(lo, hi):
        act, slope = leaky_and_slope(s.Z0[lo:hi] + s.PH[lo:hi])
        a1[lo + 1 : hi + 1, 32:64, :] = act.astype(BF)
        s.S1[lo:hi, 0:32, :] = slope

    top_rows(1, 4)
    send(*halo_adj)
    first(0)
    send(*halo_ahj)
    top_rows(0, 1)
    y = dot(take("rows")[...], take("cot")[...].reshape(256, 64)).astype(BF)
    s.CS[...] = jnp.concatenate([y[0:128], y[128:256]], 1).reshape(nh, pb, 128)
    s.COT[ha] = s.CS[ha]
    made_cot = spread("h", "cot", lambda d, h: s.CS.at[h], lambda k: s.COT.at[ha])
    take("shift2")

    def loop_taps(i, carry):
        second_taps(i, 2, 9)
        return carry

    lax.fori_loop(2, 5, loop_taps, 0)
    w2 = take("w2")
    take("eye")
    for a in range(3):
        s.W2T[a] = dot_nt(s.i_eye[...], w2[a * 288 : a * 288 + 288, :]).astype(BF)

    second_taps(1, 1, 9)
    for plane in (2, 3, 4):
        second_taps(plane, 1, 2)

    def second(i, j):
        z = None
        for a in range(3):
            term = dot(s.W2T[a], s.T2[2 * i + a, j * 192 : j * 192 + 288, :])
            z = term if z is None else z + term
        act, slope = leaky_and_slope(z)
        s.A2[i + 1, 64 + 64 * j : 128 + 64 * j, :] = act.astype(BF)
        s.S2[i, 64 * j : 64 * j + 64, :] = slope
        if i == 0 or j == 0:
            s.SS[i, 64 * j : 64 * j + 64, :] = slope.astype(BF)

    for j in (1, 2, 3):
        second(1, j)
    a2 = s.A2
    halo_bd = ("bd", a2.at[2, 64:320], a2.at[0, 64:320])
    halo_bc = ("bc", a2.at[2, 256:320], a2.at[0, 0:64])
    halo_bh = ("bh", a2.at[1:3, 256:320], a2.at[1:3, 0:64])
    halos_b = [halo_bd, halo_bc, halo_bh]
    send(*halo_bc)
    for halo_a in (halo_adi, halo_adj, halo_ac, halo_ahi, halo_ahj):
        receive(*halo_a)
    second_taps(0, 6, 9)
    second(0, 3)
    send(*halo_bh)
    for plane in (2, 3, 4):
        second_taps(plane, 0, 1)
    second(1, 0)
    send(*halo_bd)
    second_taps(0, 0, 6)
    second_taps(1, 0, 1)
    for j in (2, 1, 0):
        second(0, j)
    s2 = s.S2
    halos_s = [
        ("sd", s.SS.at[0], s.SD),
        ("sh", s.SS.at[0:2, 0:64], s.SH),
        ("sc", s.SS.at[0, 0:64], s.SC),
    ]
    for halo_s in halos_s:
        send(*halo_s, back)

    gather(made_w3)
    if nc == 2:
        other = pl.ds(pl.multiple_of((1 - core) * half, 128), half)
        to_partner("w3c", s.W3.at[:, :, my_half], s.W3.at[:, :, my_half])
        w3_other = copy(
            s.W3.at[:, :, other], s.W3.at[:, :, other], plan.sem["w3c"], (dev + 1 - 2 * core, ha)
        )

    def third_taps(blocks):
        x = [
            jnp.concatenate([a2[plane, b * 64 : b * 64 + 64, :], a2[plane, b * 64 + 128 : b * 64 + 192, :]], 1)
            for plane, b in blocks
        ]
        y = dot(jnp.concatenate(x, 0), take("taps3")[...]).astype(BF)
        for k, (plane, b) in enumerate(blocks):
            for e in range(3):
                s.T3[plane, b * 192 + e * 64 : b * 192 + e * 64 + 64, :] = y[
                    64 * k : 64 * k + 64, e * 128 : e * 128 + 128
                ]

    third_taps([(1, 1), (1, 2), (2, 1), (2, 2)])
    if nc == 2:
        w3_other.wait_recv()
    s.W3T[...] = s.W3[...].reshape(128, 1792).T
    for halo_b in halos_b:
        receive(*halo_b)
    gather(made_cot)
    third_taps([(0, 0), (0, 1), (0, 2), (1, 0), (2, 0)])
    t3 = s.T3[...].reshape(1728, 128)
    act, slope = leaky_and_slope(dot(s.W3[...].reshape(128, 1792)[:, 0:1728], t3))
    delta3 = (s.COT[...].reshape(128, 128).astype(F32) * slope).astype(BF)
    s.D3[...] = delta3
    s.OS[...] = act.astype(BF).reshape(nh, pb, 128)
    s.D3P[...] = jnp.concatenate([delta3[0:64, 0:64], delta3[64:128, 0:64]], 1)
    halos_3 = [("3d", s.D3, s.D3D), ("3h", s.D3P, s.D3H), ("3c", s.D3P, s.D3C)]
    for halo_3 in halos_3:
        send(*halo_3, back)

    lane3 = lax.broadcasted_iota(jnp.int32, (64, 128), 1)

    def third_back(parts):
        made = []
        for a, b, d in parts:
            r = a * 576 + b * 192
            x = dot(s.W3T[r : r + 192, :], d)
            even = x[64:128]
            odd = x[128:192] + jnp.where((lane3 & 63) == 63, 0.0, pltpu.roll(x[0:64], 127, 1))
            first_height = jnp.where(lane3 < 64, even, pltpu.roll(odd, 64, 1))
            made.append((first_height, jnp.where(lane3 < 64, pltpu.roll(even, 64, 1), odd)))
        return made

    b2 = s.B2
    one1, one2, two1, two2 = third_back([(1, 1, delta3), (1, 2, delta3), (2, 1, delta3), (2, 2, delta3)])
    for i, tap1, tap2 in ((0, one1, one2), (1, two1, two2)):
        b2[i, 0:64, :] = tap1[0]
        b2[i, 64:128, :] = tap2[0]
        b2[i, 128:192, :] = tap1[1]
        b2[i, 192:256, :] = tap2[1]
    g3 = dot_nt(delta3, t3)
    s.G3F[:, :, 1728:1792] = jnp.zeros((nh, pb, 64), F32)
    s.G3S[:, :, 1728:1792] = jnp.zeros((nh, pb, 64), BF)
    s.G3F[:, :, 0:1728] = g3.reshape(nh, pb, 1728)
    s.G3S[:, :, 0:1728] = g3.astype(BF).reshape(nh, pb, 1728)
    if nc == 2:
        g3c = to_partner("g3c", s.G3S.at[:, :, other], s.R3C)

    for c in range(nc):

        @pl.when(core == c)
        def _():
            total = s.G3F[:, :, c * half : c * half + half]
            if nc == 2:
                g3c.wait_recv()
                total = total + s.R3C[...].astype(F32)
            s.G3T[...] = total
            s.G3U[...] = total.astype(BF)

    made_g3h = spread("h", "g3h", lambda d, h: s.G3U.at[h], lambda k: s.R3H.at[k])

    for halo_3 in halos_3:
        receive(*halo_3, back)
    next_h = jnp.concatenate([s.D3H[:, 0:64], s.D3H[:, 64:128]], 0)
    next_c = jnp.concatenate([s.D3C[:, 0:64], s.D3C[:, 64:128]], 0)
    own = jnp.concatenate([delta3[:, 64:128], next_h], 1)
    deep = s.D3D[...]
    deep_next = jnp.concatenate([deep[:, 64:128], next_c], 1)
    beside = jnp.concatenate([next_h, next_c], 1)
    one0, two0, zero0, zero1, zero2 = third_back(
        [(1, 0, own), (2, 0, own), (0, 0, deep_next), (0, 1, deep), (0, 2, deep)]
    )
    deep0, deep1, deep2, side1, side2, side0 = third_back(
        [(1, 0, deep_next), (1, 1, deep), (1, 2, deep), (1, 1, beside), (2, 1, beside), (0, 1, beside)]
    )
    dl2 = s.DL2
    b2[0, 64:128, :] += one0[0]
    b2[0, 192:256, :] += one0[1]
    b2[0, 256:320, :] = side1[0]
    b2[1, 0:64, :] += zero1[0]
    b2[1, 64:128, :] += two0[0] + zero0[0] + zero2[0]
    b2[1, 128:192, :] += zero1[1]
    b2[1, 192:256, :] += two0[1] + zero0[1] + zero2[1]
    b2[1, 256:320, :] = side2[0] + side0[1]
    b2[2, 0:64, :] = deep1[0]
    b2[2, 64:128, :] = deep0[0] + deep2[0]
    b2[2, 128:192, :] = deep1[1]
    b2[2, 192:256, :] = deep0[1] + deep2[1]
    b2[2, 256:320, :] = side1[1]
    for halo_s in halos_s:
        receive(*halo_s, back)
    dl2[0:2, 0:256, :] = (b2[0:2, 0:256, :] * s2[...]).astype(BF)
    dl2[2, 0:256, :] = (b2[2, 0:256, :] * s.SD[...].astype(F32)).astype(BF)
    dl2[0:2, 256:320, :] = (b2[0:2, 256:320, :] * s.SH[...].astype(F32)).astype(BF)
    dl2[2, 256:320, :] = (b2[2, 256:320, :] * s.SC[...].astype(F32)).astype(BF)

    low = high = None
    none = jnp.zeros((64, 256), BF)
    for i in range(2):
        for j in (0, 2):
            x = jnp.concatenate([dl2[i, 64 * (j + t) : 64 * (j + t) + 64, :] for t in (0, 1)], 1)
            t2 = jnp.concatenate(
                [s.T2[2 * i : 2 * i + 3, 192 * (j + t) : 192 * (j + t) + 288, :].reshape(864, 128) for t in (0, 1)], 1
            )
            term = dot_nt(t2[0:512], jnp.concatenate([x, none], 0))
            low = term if low is None else low + term
            term = dot_nt(t2[512:864], jnp.concatenate([none, x], 0))
            high = term if high is None else high + term
    g2 = jnp.concatenate([low[0:352] + high, low[352:512]], 0).reshape(nc, nh, plan.r2, 128)
    s.G2F[...] = g2
    s.G2S[...] = g2.astype(BF)
    made_g2h = spread("a", "g2h", lambda d, h: s.G2S.at[d & (nc - 1), h], lambda k: s.R2H.at[k])
    made_out = spread("h", "out", lambda d, h: s.OS.at[h], lambda k: s.OR.at[ha])
    s.OR[ha] = s.OS[ha]

    lane = lax.broadcasted_iota(jnp.int32, (32, 128), 1)

    def second_back(plane, pairs, lo, hi):
        for j in range(lo // 2, hi // 2 + 1):
            y = None
            for a, i in pairs:
                term = dot(w2[a * 288 : a * 288 + 288, :], dl2[i, j * 64 : j * 64 + 64, :])
                y = term if y is None else y + term
            s.Y[j] = y
        for k in range(lo, hi):
            j = (k + 1) // 2
            d = s.Y[j, 0:96, :] + s.Y[j - 1, 192:288, :] if k % 2 else s.Y[j, 96:192, :]
            moved = jnp.where(lane < 64, pltpu.roll(d[0:32], 64, 1), pltpu.roll(d[0:32], 63, 1))
            moved = jnp.where(lane == 127, 0.0, moved)
            s.B1[plane, 32 * k : 32 * k + 32, 0:128] = d[32:64]
            s.B1[plane, 32 * k : 32 * k + 32, 128:256] = d[64:96] + moved

    planes = [[(1, 0)], [(2, 0), (0, 1)], [(1, 1)], [(2, 1), (0, 2)]]
    for plane in range(4):
        second_back(plane, planes[plane], 0, 8)

    s.G1A[...] = jnp.zeros((256, 576), F32)

    def loop_back(i, carry):
        d = (s.B1[i] * s.S1[i]).astype(BF)
        s.DL1[i] = d
        s.G1A[...] += dot_nt(d, s.T1[pl.ds(2 * i, 3)].reshape(576, 256))
        return carry

    lax.fori_loop(0, 4, loop_back, 0)
    def sum_parts(total, received, size):
        for k in range(1, size):
            total = total + received[k].astype(F32)
        return total

    gh = dot_nt(s.DL1[:, 0:32, :].reshape(128, 256), s.TH[...])
    sum_a = jnp.zeros((32, 576), F32)
    sum_b = jnp.zeros((32, 576), F32)
    for j in range(8):
        mask_a, mask_b = tap_masks(j)
        g = s.G1A[32 * j : 32 * j + 32, :]
        sum_a = sum_a + jnp.where(mask_a, g, 0.0)
        sum_b = sum_b + jnp.where(mask_b, g, 0.0)
    g1 = dot_nt(split_rows(sum_a), s.i_expand[:, 0:576])
    g1 = g1 + dot_nt(split_rows(sum_b), s.i_expand[:, 576:1152])
    for i in range(4):
        g1 = g1 + dot_nt(split_rows(gh[32 * i : 32 * i + 32]), s.i_halo[:, i * 256 : i * 256 + 192])
    g1 = g1[0:32] + g1[32:64]
    s.G1S[...] = g1.astype(BF)
    made_g1h = spread("a", "g1h", lambda d, h: s.G1S, lambda k: s.R1H.at[k])

    gather(made_g3h)
    total = sum_parts(s.G3T[ha], s.R3H, nh)
    s.P3F[...] = total
    s.P3S[...] = total.astype(BF)
    made_g3d = spread("z", "g3d", lambda d, h: s.P3S, lambda k: s.R3D.at[k])
    gather(made_g2h)
    g2 = sum_parts(s.G2F[core, ha], s.R2H, nh * nc)
    s.G2D[...] = g2.astype(BF)
    made_g2d = spread("z", "g2d", lambda d, h: s.G2D, lambda k: s.R2D.at[k])
    results = []

    def result(name, ref):
        c = pltpu.make_async_copy(getattr(s, name), ref, s.ls.at[len(results)])
        c.start()
        results.append(c)

    gather(made_out)
    result("OR", o3)
    gather(made_g1h)
    g1 = sum_parts(g1, s.R1H, nh * nc)
    s.G1D[...] = g1.astype(BF)
    made_g1d = spread("z", "g1d", lambda d, h: s.G1D, lambda k: s.R1D.at[k])
    gather(made_g2d)
    g2 = sum_parts(g2, s.R2D, nz)
    s.F2[...] = g2.astype(BF)
    s.F2H[core, ha] = g2.astype(BF)
    made_g2z = spread("a", "g2z", lambda d, h: s.F2, lambda k: s.F2H.at[core, ha])
    gather(made_g3d)
    s.F3[core] = sum_parts(s.P3F[...], s.R3D, nz)
    if nc == 2:
        to_partner("g3p", s.F3.at[core], s.F3.at[core])
        g3p = copy(s.F3.at[1 - core], s.F3.at[1 - core], plan.sem["g3p"], (dev + 1 - 2 * core, ha))
    gather(made_g1d)
    s.G1O[...] = sum_parts(g1, s.R1D, nz)
    result("G1O", g1o)
    gather(made_g2z)
    result("F2H", g2o)
    if nc == 2:
        g3p.wait_recv()
    result("F3", g3o)
    for c in results:
        c.wait()
    for ok, c in pending:
        if ok is None:
            c.wait_send()
        else:
            pl.when(ok)(c.wait_send)


def finish(plan, scales, *refs):
    nh, nc, pb = plan.nh, plan.nc, plan.pb
    out, g1, g2, g3 = refs[1:5]
    rows, o3, g1o, g2o, g3o, sem = refs[9:15]
    copied = pltpu.make_async_copy(refs[0], rows, sem.at[0])
    copied.start()
    sent = []

    def result(ref, to):
        c = pltpu.make_async_copy(ref, to, sem.at[len(sent) + 1])
        c.start()
        sent.append(c)

    x = g2[...].reshape(512, 128).astype(F32) * scales[1]
    g2o[0:512, :] = x[:, 0:64]
    g2o[512:864, :] = x[0:352, 64:128]
    result(g2o, refs[7])
    for t in range(27):
        c, r = divmod(64 * t, plan.half)
        g3o[t] = g3[c, :, r : r + 64] * scales[2]
    result(g3o, refs[8])
    x = (g1[...] * scales[0]).T
    for t in range(27):
        g1o[t] = x[4 * t : 4 * t + 4]
    result(g1o, refs[6])
    copied.wait()
    x = out[...].reshape(128, 128)
    x = jnp.concatenate([x[:, 0:64], x[:, 64:128]], 0)
    o3[...] = dot_tn(rows[...], x).astype(BF).reshape(pb, 2 * nh, 64)
    result(o3, refs[5])
    for c in sent:
        c.wait()


def local(nd, nh, volume, w_first, w_second, w_third, cotangent):
    plan = Plan(nd, nh)
    pb = plan.pb
    cells = volume.shape[1] * nd * volume.shape[2] * nh * volume.shape[3]
    scales = tuple(1.0 / math.sqrt(cells // 8**n) for n in (1, 2, 3))
    inputs = dict(
        vol=volume,
        w1=w_first.reshape(27, 4, 32),
        w2=w_second.reshape(864, 64),
        w3=jnp.transpose(w_third.reshape(27, 64, pb), (0, 2, 1)),
        cot=cotangent.reshape(pb, 2 * nh, 64),
    )
    inputs.update(zip(INPUTS[5:], constants(nh)))
    scratch = plan.scratch()
    for name in INPUTS:
        scratch["i_" + name] = pltpu.VMEM(inputs[name].shape, BF)
    names = list(scratch)
    vmem, hbm = pl.BlockSpec(memory_space=pltpu.VMEM), pl.BlockSpec(memory_space=pltpu.HBM)
    summed = pl.pallas_call(
        functools.partial(kernel, plan, names),
        out_shape=(
            pltpu.VMEM((nh, pb, 128), BF),
            pltpu.VMEM((32, 128), F32),
            pltpu.VMEM((plan.nc, nh, plan.r2, 128), BF),
            pltpu.VMEM((plan.nc, pb, plan.half), F32),
        ),
        in_specs=[hbm] * len(INPUTS),
        out_specs=(vmem,) * 4,
        scratch_shapes=[scratch[n] for n in names],
        compiler_params=pltpu.CompilerParams(
            collective_id=0 if nd * nh > 1 else None, has_side_effects=True, vmem_limit_bytes=48 * 2**20
        ),
        name="step",
    )(*[pltpu.with_memory_space_constraint(inputs[n], pltpu.HBM) for n in INPUTS])
    shapes = [((pb, 2 * nh, 64), BF), ((27, 4, 32), F32), ((864, 64), F32), ((27, pb, 64), F32)]
    out3, g1, g2, g3 = pl.pallas_call(
        functools.partial(finish, plan, scales),
        out_shape=[jax.ShapeDtypeStruct(*x) for x in shapes],
        in_specs=[hbm] + [vmem] * 4,
        out_specs=[hbm] * 4,
        scratch_shapes=[pltpu.VMEM((256, 256), BF)] + [pltpu.VMEM(*x) for x in shapes] + [pltpu.SemaphoreType.DMA((5,))],
        compiler_params=pltpu.CompilerParams(vmem_limit_bytes=48 * 2**20),
        name="finish",
    )(pltpu.with_memory_space_constraint(inputs["rows"], pltpu.HBM), *summed)
    return (
        out3.reshape(pb, 1, 2 * nh, 64),
        g1.reshape(3, 3, 3, 4, 32),
        g2.reshape(3, 3, 3, 32, 64),
        jnp.transpose(g3, (0, 2, 1)).reshape(3, 3, 3, 64, pb),
    )


def solution(mesh):
    placed = (
        P(None, "dev", "ha", None),
        P(),
        P(),
        P(None, None, None, None, "ha"),
        P("ha", "dev", None, None),
    )
    return jax.shard_map(
        functools.partial(local, mesh.shape["dev"], mesh.shape["ha"]),
        mesh=mesh,
        in_specs=placed,
        out_specs=(P("ha", "dev", None, None), P(), P(), P(None, None, None, None, "ha")),
        check_vma=False,
    )
```

time: 810 us -> 46.5 us (0.06); the launches traced: 801 us -> 46.4 us
  waiting for transfers between devices: 291 us -> 0 us
  local copies, waits for them, and re-layouts: 210 us -> 0 us
  matrix products: 168 us -> 0 us
  blocking collectives: 63.8 us -> 0 us
  Pallas kernels: 0 us -> 45.8 us
  starting transfers between devices: 34.9 us -> 0 us
  other arithmetic: 18 us -> 0 us
  between operations: 14.9 us -> 0.64 us
    psum x2 -> x0, waiting for transfers between devices: 235 us -> none  [the longest x1 147 us: local(): lax.psum((local_first, local_second), ('dev', 'ha'))]
    transpose x3 -> x0, matrix products: 118 us -> none  [weight_grad(): return jnp.transpose(result, (2, 3, 4, 0, 1))]
    broadcast_in_dim x10 -> x0, local copies, waits for them, and re-layouts: 85.8 us -> none  [the longest x3 75.3 us: weight_grad(): inputs[:, None]]
    conv_general_dilated x17 -> x0, local copies, waits for them, and re-layouts: 71.2 us -> none  [the longest x9 43.6 us: convolve(): lax.conv_general_dilated(inputs[None], kernel, (2, 2, 2), [pad_depth, pad...]
    psum x1 -> x0, blocking collectives: 63.8 us -> none  [local(): lax.psum((local_first, local_second), ('dev', 'ha'))]
    conv_general_dilated x5 -> x0, matrix products: 50.4 us -> none  [the longest x3 38.7 us: convolve(): lax.conv_general_dilated(inputs[None], kernel, (2, 2, 2), [pad_depth, pad...]
    all_gather x1 -> x0, waiting for transfers between devices: 48 us -> none  [local(): all_rows = lax.all_gather(deeper, 'ha', axis=2, tiled=True)]
    pallas_call x0 -> x2, Pallas kernels: none -> 45.8 us  [the longest x1 43.9 us: local(): pl.pallas_call(functools.partial(kernel, plan, names), out_shape=(pltpu.V...]
  transfers between devices with their start and end apart: 12 -> 0, of which waited for: 8 -> 0; matrix products, arithmetic and copies ran while one was open for 17% -> 0% of each run, Pallas kernels for 0% -> 0%
where the time goes in v2:
time: 46.5 us; the launch traced here: 46.4 us
  Pallas kernels  45.8 us (98%)
  between operations  0.64 us (1%)
    pallas_call x1, Pallas kernels, local(): pl.pallas_call(functools.partial(kernel, plan, names), out_shape=(pltpu.V...  43.9 us
    pallas_call x1, Pallas kernels, local(): pl.pallas_call(functools.partial(finish, plan, scales), out_shape=[jax.Sh...  1.83 us

profile of v2, /device:TPU:1, one launch (start us, length us, event | category | flops | bytes accessed | tf_op | source)
XLA Modules:
  0.0 46.4 jit_solution(4802629977517810852)
XLA Ops:
  0.6 43.9 %step.1 = (bf16[8,16,128]{2,1,0:T(8,128)(2,1)S(1)}, f32[32,128]{1,0:T(8,128)S(1)}, bf16[2,8,32,128]{3,2,1,0:T(8,128)(2,1)S(1)}, f32[2,16,896]{2,1,0:T(8,128)S(1)}) custom-call(bf16[4,8,16,512]{3,2,1,0:T(8,128)(2,1)} %refs_0_.2, bf16[27,4,32]{2,1,0:T(4,128)(2,1)} %bitcast.17, bf16[864,64]{1,0:T(8,128)(2,1)} %bitcast.14, bf16[27,16,64]{2,1,0:T(8,128)(2,1)} %bitcast.15, ...), custom_call_target="tpu_custom_call" | custom-call | tf_op jit(solution)/shard_map/step/pallas_call | solution.py:792
  44.6 1.8 %finish.1 = (bf16[16,16,64]{2,1,0:T(8,128)(2,1)}, f32[27,4,32]{2,1,0:T(4,128)}, f32[864,64]{1,0:T(8,128)}, f32[27,16,64]{2,1,0:T(8,128)}) custom-call(bf16[256,256]{1,0:T(8,128)(2,1)} %constant.23.clone.refs_12_.refs_0_, bf16[8,16,128]{2,1,0:T(8,128)(2,1)S(1)} %get-tuple-element.12.refs_1_, f32[32,128]{1,0:T(8,128)S(1)} %get-tuple-element.13.refs_2_, ...), custom_call_target="tpu_custom_call" | custom-call | tf_op jit(solution)/shard_map/finish/pallas_call | solution.py:809

commit v3 on v2

--- a/solution.py
+++ b/solution.py
@@ -185,7 +185,6 @@
             R1H=v((nc * nh, 32, 128), BF),
             G1D=v((32, 128), BF),
             R1D=v((self.nz, 32, 128), BF),
-            G1O=v((32, 128), F32),
             ss=pltpu.SemaphoreType.DMA((self.count,)),
             rs=pltpu.SemaphoreType.DMA((self.count,)),
             ls=pltpu.SemaphoreType.DMA((16,)),
@@ -195,7 +194,7 @@
 INPUTS = ["vol", "w1", "w2", "w3", "cot", "expand", "halo", "columns", "shift2", "taps3", "last", "eye", "rows"]
 
 
-def kernel(plan, names, *refs):
+def kernel(plan, names, scales, *refs):
     nd, nh, nc, nz, pb, mb, half = plan.nd, plan.nh, plan.nc, plan.nz, plan.pb, plan.mb, plan.half
     inputs = dict(zip(INPUTS, refs[: len(INPUTS)]))
     o3, g1o, g2o, g3o = refs[len(INPUTS) : len(INPUTS) + 4]
@@ -339,11 +338,6 @@
     blank("h", s.SH, back)
     blank("c", s.SC, back)
 
-    if nd * nh > 1:
-        pl.semaphore_wait(barrier, count)
-    halos_v = [("vd%d" % c, inputs["vol"].at[c, 7], s.V0.at[c * 16 : c * 16 + 16]) for c in range(4)]
-    for halo_v in halos_v:
-        send(*halo_v)
     w3_in = take("w3")
     for t in range(27):
         s.W3A[:, t * 64 : t * 64 + 64] = w3_in[t]
@@ -356,8 +350,11 @@
 
     vol = take("vol")
     s.HS[...] = dot(take("last")[...], vol[...].reshape(512, 512)).astype(BF)
-    halos_v = halos_v + [("vh", s.HS, s.HR.at[0]), ("vc", s.HS.at[16:32], s.HR.at[1, 16:32])]
-    for halo_v in halos_v[4:]:
+    if nd * nh > 1:
+        pl.semaphore_wait(barrier, count)
+    halos_v = [("vh", s.HS, s.HR.at[0]), ("vc", s.HS.at[16:32], s.HR.at[1, 16:32])]
+    halos_v = halos_v + [("vd%d" % c, vol.at[c, 7], s.V0.at[c * 16 : c * 16 + 16]) for c in range(4)]
+    for halo_v in halos_v:
         send(*halo_v)
 
     def taps_of(rows):
@@ -583,44 +580,26 @@
 
     made_g3h = spread("h", "g3h", lambda d, h: s.G3U.at[h], lambda k: s.R3H.at[k])
 
-    for halo_3 in halos_3:
-        receive(*halo_3, back)
+    dl2 = s.DL2
+    receive(*halos_3[1], back)
+    for halo_s in halos_s:
+        receive(*halo_s, back)
     next_h = jnp.concatenate([s.D3H[:, 0:64], s.D3H[:, 64:128]], 0)
-    next_c = jnp.concatenate([s.D3C[:, 0:64], s.D3C[:, 64:128]], 0)
     own = jnp.concatenate([delta3[:, 64:128], next_h], 1)
-    deep = s.D3D[...]
-    deep_next = jnp.concatenate([deep[:, 64:128], next_c], 1)
-    beside = jnp.concatenate([next_h, next_c], 1)
-    one0, two0, zero0, zero1, zero2 = third_back(
-        [(1, 0, own), (2, 0, own), (0, 0, deep_next), (0, 1, deep), (0, 2, deep)]
-    )
-    deep0, deep1, deep2, side1, side2, side0 = third_back(
-        [(1, 0, deep_next), (1, 1, deep), (1, 2, deep), (1, 1, beside), (2, 1, beside), (0, 1, beside)]
-    )
-    dl2 = s.DL2
+    one0, two0, side1, side2 = third_back([(1, 0, own), (2, 0, own), (1, 1, own), (2, 1, own)])
     b2[0, 64:128, :] += one0[0]
     b2[0, 192:256, :] += one0[1]
-    b2[0, 256:320, :] = side1[0]
-    b2[1, 0:64, :] += zero1[0]
-    b2[1, 64:128, :] += two0[0] + zero0[0] + zero2[0]
-    b2[1, 128:192, :] += zero1[1]
-    b2[1, 192:256, :] += two0[1] + zero0[1] + zero2[1]
-    b2[1, 256:320, :] = side2[0] + side0[1]
-    b2[2, 0:64, :] = deep1[0]
-    b2[2, 64:128, :] = deep0[0] + deep2[0]
-    b2[2, 128:192, :] = deep1[1]
-    b2[2, 192:256, :] = deep0[1] + deep2[1]
-    b2[2, 256:320, :] = side1[1]
-    for halo_s in halos_s:
-        receive(*halo_s, back)
-    dl2[0:2, 0:256, :] = (b2[0:2, 0:256, :] * s2[...]).astype(BF)
-    dl2[2, 0:256, :] = (b2[2, 0:256, :] * s.SD[...].astype(F32)).astype(BF)
-    dl2[0:2, 256:320, :] = (b2[0:2, 256:320, :] * s.SH[...].astype(F32)).astype(BF)
-    dl2[2, 256:320, :] = (b2[2, 256:320, :] * s.SC[...].astype(F32)).astype(BF)
-
-    low = high = None
+    b2[0, 256:320, :] = side1[1]
+    b2[1, 64:128, :] += two0[0]
+    b2[1, 192:256, :] += two0[1]
+    b2[1, 256:320, :] = side2[1]
+    dl2[0, 0:256, :] = (b2[0, 0:256, :] * s2[0]).astype(BF)
+    dl2[0, 256:320, :] = (b2[0, 256:320, :] * s.SH[0].astype(F32)).astype(BF)
+
     none = jnp.zeros((64, 256), BF)
-    for i in range(2):
+
+    def second_grad(i):
+        low = high = None
         for j in (0, 2):
             x = jnp.concatenate([dl2[i, 64 * (j + t) : 64 * (j + t) + 64, :] for t in (0, 1)], 1)
             t2 = jnp.concatenate(
@@ -630,23 +609,18 @@
             low = term if low is None else low + term
             term = dot_nt(t2[512:864], jnp.concatenate([none, x], 0))
             high = term if high is None else high + term
-    g2 = jnp.concatenate([low[0:352] + high, low[352:512]], 0).reshape(nc, nh, plan.r2, 128)
-    s.G2F[...] = g2
-    s.G2S[...] = g2.astype(BF)
-    made_g2h = spread("a", "g2h", lambda d, h: s.G2S.at[d & (nc - 1), h], lambda k: s.R2H.at[k])
-    made_out = spread("h", "out", lambda d, h: s.OS.at[h], lambda k: s.OR.at[ha])
-    s.OR[ha] = s.OS[ha]
+        return jnp.concatenate([low[0:352] + high, low[352:512]], 0).reshape(nc, nh, plan.r2, 128)
 
     lane = lax.broadcasted_iota(jnp.int32, (32, 128), 1)
 
-    def second_back(plane, pairs, lo, hi):
-        for j in range(lo // 2, hi // 2 + 1):
+    def second_back(plane, pairs):
+        for j in range(5):
             y = None
             for a, i in pairs:
                 term = dot(w2[a * 288 : a * 288 + 288, :], dl2[i, j * 64 : j * 64 + 64, :])
                 y = term if y is None else y + term
             s.Y[j] = y
-        for k in range(lo, hi):
+        for k in range(8):
             j = (k + 1) // 2
             d = s.Y[j, 0:96, :] + s.Y[j - 1, 192:288, :] if k % 2 else s.Y[j, 96:192, :]
             moved = jnp.where(lane < 64, pltpu.roll(d[0:32], 64, 1), pltpu.roll(d[0:32], 63, 1))
@@ -654,9 +628,43 @@
             s.B1[plane, 32 * k : 32 * k + 32, 0:128] = d[32:64]
             s.B1[plane, 32 * k : 32 * k + 32, 128:256] = d[64:96] + moved
 
-    planes = [[(1, 0)], [(2, 0), (0, 1)], [(1, 1)], [(2, 1), (0, 2)]]
-    for plane in range(4):
-        second_back(plane, planes[plane], 0, 8)
+    s.G2F[...] = second_grad(0)
+    second_back(0, [(1, 0)])
+    receive(*halos_3[0], back)
+    receive(*halos_3[2], back)
+    next_c = jnp.concatenate([s.D3C[:, 0:64], s.D3C[:, 64:128]], 0)
+    deep = s.D3D[...]
+    deep_next = jnp.concatenate([deep[:, 64:128], next_c], 1)
+    zero0, zero1, zero2, side0 = third_back(
+        [(0, 0, deep_next), (0, 1, deep), (0, 2, deep), (0, 1, deep_next)]
+    )
+    b2[1, 0:64, :] += zero1[0]
+    b2[1, 64:128, :] += zero0[0] + zero2[0]
+    b2[1, 128:192, :] += zero1[1]
+    b2[1, 192:256, :] += zero0[1] + zero2[1]
+    b2[1, 256:320, :] += side0[1]
+    dl2[1, 0:256, :] = (b2[1, 0:256, :] * s2[1]).astype(BF)
+    g2 = s.G2F[...] + second_grad(1)
+    s.G2F[...] = g2
+    s.G2S[...] = g2.astype(BF)
+    made_g2h = spread("a", "g2h", lambda d, h: s.G2S.at[d & (nc - 1), h], lambda k: s.R2H.at[k])
+    made_out = spread("h", "out", lambda d, h: s.OS.at[h], lambda k: s.OR.at[ha])
+    s.OR[ha] = s.OS[ha]
+    deep0, deep1, deep2, side3 = third_back(
+        [(1, 0, deep_next), (1, 1, deep), (1, 2, deep), (1, 1, deep_next)]
+    )
+    b2[2, 0:64, :] = deep1[0]
+    b2[2, 64:128, :] = deep0[0] + deep2[0]
+    b2[2, 128:192, :] = deep1[1]
+    b2[2, 192:256, :] = deep0[1] + deep2[1]
+    b2[2, 256:320, :] = side3[1]
+    dl2[2, 0:256, :] = (b2[2, 0:256, :] * s.SD[...].astype(F32)).astype(BF)
+    dl2[1, 256:320, :] = (b2[1, 256:320, :] * s.SH[1].astype(F32)).astype(BF)
+    dl2[2, 256:320, :] = (b2[2, 256:320, :] * s.SC[...].astype(F32)).astype(BF)
+
+    second_back(1, [(2, 0), (0, 1)])
+    second_back(2, [(1, 1)])
+    second_back(3, [(2, 1), (0, 2)])
 
     s.G1A[...] = jnp.zeros((256, 576), F32)
 
@@ -697,15 +705,10 @@
     g2 = sum_parts(s.G2F[core, ha], s.R2H, nh * nc)
     s.G2D[...] = g2.astype(BF)
     made_g2d = spread("z", "g2d", lambda d, h: s.G2D, lambda k: s.R2D.at[k])
-    results = []
-
-    def result(name, ref):
-        c = pltpu.make_async_copy(getattr(s, name), ref, s.ls.at[len(results)])
-        c.start()
-        results.append(c)
-
     gather(made_out)
-    result("OR", o3)
+    x = s.OR[...].reshape(128, 128)
+    x = jnp.concatenate([x[:, 0:64], x[:, 64:128]], 0)
+    o3[...] = dot_tn(s.i_rows[...], x).astype(BF).reshape(pb, 2 * nh, 64)
     gather(made_g1h)
     g1 = sum_parts(g1, s.R1H, nh * nc)
     s.G1D[...] = g1.astype(BF)
@@ -721,15 +724,18 @@
         to_partner("g3p", s.F3.at[core], s.F3.at[core])
         g3p = copy(s.F3.at[1 - core], s.F3.at[1 - core], plan.sem["g3p"], (dev + 1 - 2 * core, ha))
     gather(made_g1d)
-    s.G1O[...] = sum_parts(g1, s.R1D, nz)
-    result("G1O", g1o)
-    gather(made_g2z)
-    result("F2H", g2o)
+    x = (sum_parts(g1, s.R1D, nz) * scales[0]).T
+    for t in range(27):
+        g1o[t] = x[4 * t : 4 * t + 4]
     if nc == 2:
         g3p.wait_recv()
-    result("F3", g3o)
-    for c in results:
-        c.wait()
+    for t in range(27):
+        c, r = divmod(64 * t, half)
+        g3o[t] = s.F3[c, :, r : r + 64] * scales[2]
+    gather(made_g2z)
+    x = s.F2H[...].reshape(512, 128).astype(F32) * scales[1]
+    g2o[0:512, :] = x[:, 0:64]
+    g2o[512:864, :] = x[0:352, 64:128]
     for ok, c in pending:
         if ok is None:
             c.wait_send()
@@ -737,37 +743,11 @@
             pl.when(ok)(c.wait_send)
 
 
-def finish(plan, scales, *refs):
-    nh, nc, pb = plan.nh, plan.nc, plan.pb
-    out, g1, g2, g3 = refs[1:5]
-    rows, o3, g1o, g2o, g3o, sem = refs[9:15]
-    copied = pltpu.make_async_copy(refs[0], rows, sem.at[0])
-    copied.start()
-    sent = []
-
-    def result(ref, to):
-        c = pltpu.make_async_copy(ref, to, sem.at[len(sent) + 1])
+def finish(*refs):
+    copies = [pltpu.make_async_copy(refs[k], refs[4 + k], refs[8].at[k]) for k in range(4)]
+    for c in copies:
         c.start()
-        sent.append(c)
-
-    x = g2[...].reshape(512, 128).astype(F32) * scales[1]
-    g2o[0:512, :] = x[:, 0:64]
-    g2o[512:864, :] = x[0:352, 64:128]
-    result(g2o, refs[7])
-    for t in range(27):
-        c, r = divmod(64 * t, plan.half)
-        g3o[t] = g3[c, :, r : r + 64] * scales[2]
-    result(g3o, refs[8])
-    x = (g1[...] * scales[0]).T
-    for t in range(27):
-        g1o[t] = x[4 * t : 4 * t + 4]
-    result(g1o, refs[6])
-    copied.wait()
-    x = out[...].reshape(128, 128)
-    x = jnp.concatenate([x[:, 0:64], x[:, 64:128]], 0)
-    o3[...] = dot_tn(rows[...], x).astype(BF).reshape(pb, 2 * nh, 64)
-    result(o3, refs[5])
-    for c in sent:
+    for c in copies:
         c.wait()
 
 
@@ -789,32 +769,27 @@
         scratch["i_" + name] = pltpu.VMEM(inputs[name].shape, BF)
     names = list(scratch)
     vmem, hbm = pl.BlockSpec(memory_space=pltpu.VMEM), pl.BlockSpec(memory_space=pltpu.HBM)
-    summed = pl.pallas_call(
-        functools.partial(kernel, plan, names),
-        out_shape=(
-            pltpu.VMEM((nh, pb, 128), BF),
-            pltpu.VMEM((32, 128), F32),
-            pltpu.VMEM((plan.nc, nh, plan.r2, 128), BF),
-            pltpu.VMEM((plan.nc, pb, plan.half), F32),
-        ),
+    shapes = [((pb, 2 * nh, 64), BF), ((27, 4, 32), F32), ((864, 64), F32), ((27, pb, 64), F32)]
+    made = pl.pallas_call(
+        functools.partial(kernel, plan, names, scales),
+        out_shape=[pltpu.VMEM(*x) for x in shapes],
         in_specs=[hbm] * len(INPUTS),
-        out_specs=(vmem,) * 4,
+        out_specs=[vmem] * 4,
         scratch_shapes=[scratch[n] for n in names],
         compiler_params=pltpu.CompilerParams(
             collective_id=0 if nd * nh > 1 else None, has_side_effects=True, vmem_limit_bytes=48 * 2**20
         ),
         name="step",
     )(*[pltpu.with_memory_space_constraint(inputs[n], pltpu.HBM) for n in INPUTS])
-    shapes = [((pb, 2 * nh, 64), BF), ((27, 4, 32), F32), ((864, 64), F32), ((27, pb, 64), F32)]
     out3, g1, g2, g3 = pl.pallas_call(
-        functools.partial(finish, plan, scales),
+        finish,
         out_shape=[jax.ShapeDtypeStruct(*x) for x in shapes],
-        in_specs=[hbm] + [vmem] * 4,
+        in_specs=[vmem] * 4,
         out_specs=[hbm] * 4,
-        scratch_shapes=[pltpu.VMEM((256, 256), BF)] + [pltpu.VMEM(*x) for x in shapes] + [pltpu.SemaphoreType.DMA((5,))],
+        scratch_shapes=[pltpu.SemaphoreType.DMA((4,))],
         compiler_params=pltpu.CompilerParams(vmem_limit_bytes=48 * 2**20),
         name="finish",
-    )(pltpu.with_memory_space_constraint(inputs["rows"], pltpu.HBM), *summed)
+    )(*made)
     return (
         out3.reshape(pb, 1, 2 * nh, 64),
         g1.reshape(3, 3, 3, 4, 32),

time: 46.5 us -> 44.3 us (0.953)
  Pallas kernels: 45.8 us -> 43.5 us
    pallas_call x2, Pallas kernels: 45.8 us -> 43.5 us  [the longest x1 42.6 us: local(): pl.pallas_call(functools.partial(kernel, plan, names, scales), out_shape=...]
where the time goes in v3:
time: 44.3 us; the launch traced here: 44.2 us
  Pallas kernels  43.5 us (98%)
  between operations  0.64 us (1%)
    pallas_call x1, Pallas kernels, local(): pl.pallas_call(functools.partial(kernel, plan, names, scales), out_shape=...  42.6 us
    pallas_call x1, Pallas kernels, local(): pl.pallas_call(finish, out_shape=[jax.ShapeDtypeStruct(*x) for x in shape...  0.91 us

profile of v3, /device:TPU:1, one launch (start us, length us, event | category | flops | bytes accessed | tf_op | source)
XLA Modules:
  0.0 44.2 jit_solution(15447503084948480185)
XLA Ops:
  0.6 42.6 %step.1 = (bf16[16,16,64]{2,1,0:T(8,128)(2,1)S(1)}, f32[27,4,32]{2,1,0:T(4,128)S(1)}, f32[864,64]{1,0:T(8,128)S(1)}, f32[27,16,64]{2,1,0:T(8,128)S(1)}) custom-call(bf16[4,8,16,512]{3,2,1,0:T(8,128)(2,1)} %refs_0_.1, bf16[27,4,32]{2,1,0:T(4,128)(2,1)} %bitcast.17, bf16[864,64]{1,0:T(8,128)(2,1)} %bitcast.14, bf16[27,16,64]{2,1,0:T(8,128)(2,1)} %bitcast.15, ...), custom_call_target="tpu_custom_call" | custom-call | tf_op jit(solution)/shard_map/step/pallas_call | solution.py:773
  43.2 0.9 %finish.1 = (bf16[16,16,64]{2,1,0:T(8,128)(2,1)}, f32[27,4,32]{2,1,0:T(4,128)}, f32[864,64]{1,0:T(8,128)}, f32[27,16,64]{2,1,0:T(8,128)}) custom-call(bf16[16,16,64]{2,1,0:T(8,128)(2,1)S(1)} %get-tuple-element.12.refs_0_, f32[27,4,32]{2,1,0:T(4,128)S(1)} %get-tuple-element.13.refs_1_, f32[864,64]{1,0:T(8,128)S(1)} %get-tuple-element.14.refs_2_, ...), custom_call_target="tpu_custom_call" | custom-call | tf_op jit(solution)/shard_map/finish/pallas_call | solution.py:784

commit v4 on v3

--- a/solution.py
+++ b/solution.py
@@ -62,7 +62,7 @@
             for e in range(3):
                 for c in range(4):
                     row = (a * 9 + e) * 4 + c
-                    halo[row, i * 256 + e * 64 + s * 32 + plane * 4 + c] = 1
+                    halo[row, i * 256 + s * 96 + e * 32 + plane * 4 + c] = 1
     columns = np.zeros((512, 768), np.float32)
     for e in range(3):
         for p in range(256):
@@ -132,7 +132,8 @@
             TH=v((192, 256), BF),
             W1F=v((128, 32), F32),
             WT=v((256, 576), BF),
-            WH=v((4, 32, 192), BF),
+            WH=v((4, 32, 96), BF),
+            WC=v((32, 96), BF),
             PH=v((4, 32, 256), F32),
             Z0=v((4, 32, 256), F32),
             A1=v((5, 288, 256), BF),
@@ -272,6 +273,13 @@
     }
     pending = []
 
+    def finish_sends(copies):
+        for ok, c in copies:
+            if ok is None:
+                c.wait_send()
+            else:
+                pl.when(ok)(c.wait_send)
+
     def send(name, src, dst, table=routes):
         can_send, can_receive, exists, target = table[name[1]]
         if not exists:
@@ -294,9 +302,9 @@
         def _():
             ref[...] = jnp.zeros(ref.shape, ref.dtype)
 
-    def spread(group, name, src_of, dst, valid_send=None):
+    def spread(group, name, src_of, dst, valid_send=None, part=(1, 99)):
         made = []
-        for k in range(1, sizes[group]):
+        for k in range(part[0], min(part[1], sizes[group])):
             target = peer_of(group, k)
             c = copy(src_of(*target), dst(k), plan.sem[name] + k - 1, target)
             ok = None if valid_send is None else valid_send(target[0])
@@ -385,7 +393,8 @@
         s.WT[j * 32 : j * 32 + 32, :] = jnp.where(mask_a, base_a, jnp.where(mask_b, base_b, 0.0)).astype(BF)
     edge = dot_tn(w1b, take("halo")[...]).astype(BF)
     for i in range(4):
-        s.WH[i] = edge[:, i * 256 : i * 256 + 192]
+        s.WH[i] = edge[:, i * 256 : i * 256 + 96]
+    s.WC[...] = edge[:, 96:192]
 
     def first(i):
         z = dot(s.WT[...], s.T1[pl.ds(2 * i, 3)].reshape(576, 256))
@@ -421,14 +430,17 @@
     send(*halo_ahi)
 
     my_half = pl.ds(pl.multiple_of(core * half, 128), half)
-    made_w3 = spread("h", "w3", lambda d, h: s.W3A.at[:, my_half], lambda k: s.W3.at[ha, :, my_half])
+    made_w3 = spread(
+        "h", "w3", lambda d, h: s.W3A.at[:, my_half], lambda k: s.W3.at[ha, :, my_half], part=(1, 4)
+    )
+    halo_vc = halos_v.pop(1)
     for halo_v in halos_v:
         receive(*halo_v)
-    edges = taps_of(jnp.concatenate([s.V0[...], s.HR[...].reshape(64, 512)], 0))
+    edges = taps_of(jnp.concatenate([s.V0[...], s.HR[0]], 0))
     for e in range(3):
         s.T1[0, e * 64 : e * 64 + 64, :] = edges[0:64, e * 256 : e * 256 + 256]
-        s.TH[e * 64 : e * 64 + 64, :] = edges[64:128, e * 256 : e * 256 + 256]
-    s.PH[...] = dot(s.WH[...].reshape(128, 192), s.TH[...]).reshape(4, 32, 256)
+        s.TH[e * 32 : e * 32 + 32, :] = edges[64:96, e * 256 : e * 256 + 256]
+    s.PH[...] = dot(s.WH[...].reshape(128, 96), s.TH[0:96, :]).reshape(4, 32, 256)
 
     def top_rows(lo, hi):
         act, slope = leaky_and_slope(s.Z0[lo:hi] + s.PH[lo:hi])
@@ -439,7 +451,9 @@
     send(*halo_adj)
     first(0)
     send(*halo_ahj)
-    top_rows(0, 1)
+    made_w3 += spread(
+        "h", "w3", lambda d, h: s.W3A.at[:, my_half], lambda k: s.W3.at[ha, :, my_half], part=(4, 99)
+    )
     y = dot(take("rows")[...], take("cot")[...].reshape(256, 64)).astype(BF)
     s.CS[...] = jnp.concatenate([y[0:128], y[128:256]], 1).reshape(nh, pb, 128)
     s.COT[ha] = s.CS[ha]
@@ -456,6 +470,12 @@
     for a in range(3):
         s.W2T[a] = dot_nt(s.i_eye[...], w2[a * 288 : a * 288 + 288, :]).astype(BF)
 
+    receive(*halo_vc)
+    edges = taps_of(s.HR[1])
+    for e in range(3):
+        s.TH[96 + e * 32 : 128 + e * 32, :] = edges[:, e * 256 : e * 256 + 256]
+    s.PH[0] += dot(s.WC[...], s.TH[96:192, :])
+    top_rows(0, 1)
     second_taps(1, 1, 9)
     for plane in (2, 3, 4):
         second_taps(plane, 1, 2)
@@ -501,14 +521,6 @@
     for halo_s in halos_s:
         send(*halo_s, back)
 
-    gather(made_w3)
-    if nc == 2:
-        other = pl.ds(pl.multiple_of((1 - core) * half, 128), half)
-        to_partner("w3c", s.W3.at[:, :, my_half], s.W3.at[:, :, my_half])
-        w3_other = copy(
-            s.W3.at[:, :, other], s.W3.at[:, :, other], plan.sem["w3c"], (dev + 1 - 2 * core, ha)
-        )
-
     def third_taps(blocks):
         x = [
             jnp.concatenate([a2[plane, b * 64 : b * 64 + 64, :], a2[plane, b * 64 + 128 : b * 64 + 192, :]], 1)
@@ -522,13 +534,20 @@
                 ]
 
     third_taps([(1, 1), (1, 2), (2, 1), (2, 2)])
+    gather(made_w3)
     if nc == 2:
-        w3_other.wait_recv()
-    s.W3T[...] = s.W3[...].reshape(128, 1792).T
+        other = pl.ds(pl.multiple_of((1 - core) * half, 128), half)
+        to_partner("w3c", s.W3.at[:, :, my_half], s.W3.at[:, :, my_half])
+        w3_other = copy(
+            s.W3.at[:, :, other], s.W3.at[:, :, other], plan.sem["w3c"], (dev + 1 - 2 * core, ha)
+        )
+
     for halo_b in halos_b:
         receive(*halo_b)
     gather(made_cot)
     third_taps([(0, 0), (0, 1), (0, 2), (1, 0), (2, 0)])
+    if nc == 2:
+        w3_other.wait_recv()
     t3 = s.T3[...].reshape(1728, 128)
     act, slope = leaky_and_slope(dot(s.W3[...].reshape(128, 1792)[:, 0:1728], t3))
     delta3 = (s.COT[...].reshape(128, 128).astype(F32) * slope).astype(BF)
@@ -552,6 +571,7 @@
             made.append((first_height, jnp.where(lane3 < 64, pltpu.roll(even, 64, 1), odd)))
         return made
 
+    s.W3T[...] = s.W3[...].reshape(128, 1792).T
     b2 = s.B2
     one1, one2, two1, two2 = third_back([(1, 1, delta3), (1, 2, delta3), (2, 1, delta3), (2, 2, delta3)])
     for i, tap1, tap2 in ((0, one1, one2), (1, two1, two2)):
@@ -598,17 +618,13 @@
 
     none = jnp.zeros((64, 256), BF)
 
-    def second_grad(i):
-        low = high = None
-        for j in (0, 2):
-            x = jnp.concatenate([dl2[i, 64 * (j + t) : 64 * (j + t) + 64, :] for t in (0, 1)], 1)
-            t2 = jnp.concatenate(
-                [s.T2[2 * i : 2 * i + 3, 192 * (j + t) : 192 * (j + t) + 288, :].reshape(864, 128) for t in (0, 1)], 1
-            )
-            term = dot_nt(t2[0:512], jnp.concatenate([x, none], 0))
-            low = term if low is None else low + term
-            term = dot_nt(t2[512:864], jnp.concatenate([none, x], 0))
-            high = term if high is None else high + term
+    def second_grad(i, j):
+        x = jnp.concatenate([dl2[i, 64 * (j + t) : 64 * (j + t) + 64, :] for t in (0, 1)], 1)
+        t2 = jnp.concatenate(
+            [s.T2[2 * i : 2 * i + 3, 192 * (j + t) : 192 * (j + t) + 288, :].reshape(864, 128) for t in (0, 1)], 1
+        )
+        low = dot_nt(t2[0:512], jnp.concatenate([x, none], 0))
+        high = dot_nt(t2[512:864], jnp.concatenate([none, x], 0))
         return jnp.concatenate([low[0:352] + high, low[352:512]], 0).reshape(nc, nh, plan.r2, 128)
 
     lane = lax.broadcasted_iota(jnp.int32, (32, 128), 1)
@@ -628,23 +644,24 @@
             s.B1[plane, 32 * k : 32 * k + 32, 0:128] = d[32:64]
             s.B1[plane, 32 * k : 32 * k + 32, 128:256] = d[64:96] + moved
 
-    s.G2F[...] = second_grad(0)
+    s.G2F[...] = second_grad(0, 0) + second_grad(0, 2)
     second_back(0, [(1, 0)])
     receive(*halos_3[0], back)
+    deep = s.D3D[...]
+    zero0, zero1, zero2 = third_back([(0, 0, deep), (0, 1, deep), (0, 2, deep)])
+    b2[1, 0:64, :] += zero1[0]
+    b2[1, 64:128, :] += zero0[1] + zero2[0]
+    b2[1, 128:192, :] += zero1[1]
+    dl2[1, 0:192, :] = (b2[1, 0:192, :] * s2[1, 0:192, :]).astype(BF)
+    s.G2F[...] += second_grad(1, 0)
     receive(*halos_3[2], back)
     next_c = jnp.concatenate([s.D3C[:, 0:64], s.D3C[:, 64:128]], 0)
-    deep = s.D3D[...]
     deep_next = jnp.concatenate([deep[:, 64:128], next_c], 1)
-    zero0, zero1, zero2, side0 = third_back(
-        [(0, 0, deep_next), (0, 1, deep), (0, 2, deep), (0, 1, deep_next)]
-    )
-    b2[1, 0:64, :] += zero1[0]
-    b2[1, 64:128, :] += zero0[0] + zero2[0]
-    b2[1, 128:192, :] += zero1[1]
-    b2[1, 192:256, :] += zero0[1] + zero2[1]
+    corner0, side0 = third_back([(0, 0, deep_next), (0, 1, deep_next)])
+    b2[1, 192:256, :] += corner0[1] + zero2[1]
     b2[1, 256:320, :] += side0[1]
-    dl2[1, 0:256, :] = (b2[1, 0:256, :] * s2[1]).astype(BF)
-    g2 = s.G2F[...] + second_grad(1)
+    dl2[1, 192:256, :] = (b2[1, 192:256, :] * s2[1, 192:256, :]).astype(BF)
+    g2 = s.G2F[...] + second_grad(1, 2)
     s.G2F[...] = g2
     s.G2S[...] = g2.astype(BF)
     made_g2h = spread("a", "g2h", lambda d, h: s.G2S.at[d & (nc - 1), h], lambda k: s.R2H.at[k])
@@ -717,6 +734,7 @@
     g2 = sum_parts(g2, s.R2D, nz)
     s.F2[...] = g2.astype(BF)
     s.F2H[core, ha] = g2.astype(BF)
+    settled = len(pending)
     made_g2z = spread("a", "g2z", lambda d, h: s.F2, lambda k: s.F2H.at[core, ha])
     gather(made_g3d)
     s.F3[core] = sum_parts(s.P3F[...], s.R3D, nz)
@@ -732,15 +750,12 @@
     for t in range(27):
         c, r = divmod(64 * t, half)
         g3o[t] = s.F3[c, :, r : r + 64] * scales[2]
+    finish_sends(pending[:settled])
     gather(made_g2z)
     x = s.F2H[...].reshape(512, 128).astype(F32) * scales[1]
     g2o[0:512, :] = x[:, 0:64]
     g2o[512:864, :] = x[0:352, 64:128]
-    for ok, c in pending:
-        if ok is None:
-            c.wait_send()
-        else:
-            pl.when(ok)(c.wait_send)
+    finish_sends(pending[settled:])
 
 
 def finish(*refs):

time: 44.3 us -> 43.2 us (0.975)
  Pallas kernels: 43.5 us -> 42.4 us
    pallas_call x1, Pallas kernels: 42.6 us -> 41.5 us  [local(): pl.pallas_call(functools.partial(kernel, plan, names, scales), out_shape=...]
where the time goes in v4:
time: 43.2 us; the launch traced here: 43.1 us
  Pallas kernels  42.4 us (98%)
  between operations  0.64 us (1%)
    pallas_call x1, Pallas kernels, local(): pl.pallas_call(functools.partial(kernel, plan, names, scales), out_shape=...  41.5 us
    pallas_call x1, Pallas kernels, local(): pl.pallas_call(finish, out_shape=[jax.ShapeDtypeStruct(*x) for x in shape...  0.91 us

profile of v4, /device:TPU:1, one launch (start us, length us, event | category | flops | bytes accessed | tf_op | source)
XLA Modules:
  0.0 43.1 jit_solution(3424955636912836676)
XLA Ops:
  0.6 41.5 %step.1 = (bf16[16,16,64]{2,1,0:T(8,128)(2,1)S(1)}, f32[27,4,32]{2,1,0:T(4,128)S(1)}, f32[864,64]{1,0:T(8,128)S(1)}, f32[27,16,64]{2,1,0:T(8,128)S(1)}) custom-call(bf16[4,8,16,512]{3,2,1,0:T(8,128)(2,1)} %refs_0_.1, bf16[27,4,32]{2,1,0:T(4,128)(2,1)} %bitcast.17, bf16[864,64]{1,0:T(8,128)(2,1)} %bitcast.14, bf16[27,16,64]{2,1,0:T(8,128)(2,1)} %bitcast.15, ...), custom_call_target="tpu_custom_call" | custom-call | tf_op jit(solution)/shard_map/step/pallas_call | solution.py:788
  42.2 0.9 %finish.1 = (bf16[16,16,64]{2,1,0:T(8,128)(2,1)}, f32[27,4,32]{2,1,0:T(4,128)}, f32[864,64]{1,0:T(8,128)}, f32[27,16,64]{2,1,0:T(8,128)}) custom-call(bf16[16,16,64]{2,1,0:T(8,128)(2,1)S(1)} %get-tuple-element.12.refs_0_, f32[27,4,32]{2,1,0:T(4,128)S(1)} %get-tuple-element.13.refs_1_, f32[864,64]{1,0:T(8,128)S(1)} %get-tuple-element.14.refs_2_, ...), custom_call_target="tpu_custom_call" | custom-call | tf_op jit(solution)/shard_map/finish/pallas_call | solution.py:799

commit v5 on v4

--- a/solution.py
+++ b/solution.py
@@ -431,7 +431,7 @@
 
     my_half = pl.ds(pl.multiple_of(core * half, 128), half)
     made_w3 = spread(
-        "h", "w3", lambda d, h: s.W3A.at[:, my_half], lambda k: s.W3.at[ha, :, my_half], part=(1, 4)
+        "h", "w3", lambda d, h: s.W3A.at[:, my_half], lambda k: s.W3.at[ha, :, my_half], part=(1, 5)
     )
     halo_vc = halos_v.pop(1)
     for halo_v in halos_v:
@@ -452,7 +452,7 @@
     first(0)
     send(*halo_ahj)
     made_w3 += spread(
-        "h", "w3", lambda d, h: s.W3A.at[:, my_half], lambda k: s.W3.at[ha, :, my_half], part=(4, 99)
+        "h", "w3", lambda d, h: s.W3A.at[:, my_half], lambda k: s.W3.at[ha, :, my_half], part=(5, 99)
     )
     y = dot(take("rows")[...], take("cot")[...].reshape(256, 64)).astype(BF)
     s.CS[...] = jnp.concatenate([y[0:128], y[128:256]], 1).reshape(nh, pb, 128)

time: 43.2 us -> 43.2 us (level)
  no operation moved by 1% of the time
where the time goes in v5:
time: 43.2 us; the launch traced here: 43.1 us
  Pallas kernels  42.4 us (98%)
  between operations  0.64 us (1%)
    pallas_call x1, Pallas kernels, local(): pl.pallas_call(functools.partial(kernel, plan, names, scales), out_shape=...  41.5 us
    pallas_call x1, Pallas kernels, local(): pl.pallas_call(finish, out_shape=[jax.ShapeDtypeStruct(*x) for x in shape...  0.91 us

profile of v5, /device:TPU:1, one launch (start us, length us, event | category | flops | bytes accessed | tf_op | source)
XLA Modules:
  0.0 43.1 jit_solution(71343989460581000)
XLA Ops:
  0.6 41.5 %step.1 = (bf16[16,16,64]{2,1,0:T(8,128)(2,1)S(1)}, f32[27,4,32]{2,1,0:T(4,128)S(1)}, f32[864,64]{1,0:T(8,128)S(1)}, f32[27,16,64]{2,1,0:T(8,128)S(1)}) custom-call(bf16[4,8,16,512]{3,2,1,0:T(8,128)(2,1)} %refs_0_.1, bf16[27,4,32]{2,1,0:T(4,128)(2,1)} %bitcast.17, bf16[864,64]{1,0:T(8,128)(2,1)} %bitcast.14, bf16[27,16,64]{2,1,0:T(8,128)(2,1)} %bitcast.15, ...), custom_call_target="tpu_custom_call" | custom-call | tf_op jit(solution)/shard_map/step/pallas_call | solution.py:788
  42.2 0.9 %finish.1 = (bf16[16,16,64]{2,1,0:T(8,128)(2,1)}, f32[27,4,32]{2,1,0:T(4,128)}, f32[864,64]{1,0:T(8,128)}, f32[27,16,64]{2,1,0:T(8,128)}) custom-call(bf16[16,16,64]{2,1,0:T(8,128)(2,1)S(1)} %get-tuple-element.12.refs_0_, f32[27,4,32]{2,1,0:T(4,128)S(1)} %get-tuple-element.13.refs_1_, f32[864,64]{1,0:T(8,128)S(1)} %get-tuple-element.14.refs_2_, ...), custom_call_target="tpu_custom_call" | custom-call | tf_op jit(solution)/shard_map/finish/pallas_call | solution.py:799

commit v6 on v4

--- a/solution.py
+++ b/solution.py
@@ -665,8 +665,6 @@
     s.G2F[...] = g2
     s.G2S[...] = g2.astype(BF)
     made_g2h = spread("a", "g2h", lambda d, h: s.G2S.at[d & (nc - 1), h], lambda k: s.R2H.at[k])
-    made_out = spread("h", "out", lambda d, h: s.OS.at[h], lambda k: s.OR.at[ha])
-    s.OR[ha] = s.OS[ha]
     deep0, deep1, deep2, side3 = third_back(
         [(1, 0, deep_next), (1, 1, deep), (1, 2, deep), (1, 1, deep_next)]
     )
@@ -683,6 +681,8 @@
     second_back(2, [(1, 1)])
     second_back(3, [(2, 1), (0, 2)])
 
+    made_out = spread("h", "out", lambda d, h: s.OS.at[h], lambda k: s.OR.at[ha])
+    s.OR[ha] = s.OS[ha]
     s.G1A[...] = jnp.zeros((256, 576), F32)
 
     def loop_back(i, carry):

time: 43.2 us -> 43.2 us (level)
  no operation moved by 1% of the time
where the time goes in v6:
time: 43.2 us; the launch traced here: 43.1 us
  Pallas kernels  42.4 us (98%)
  between operations  0.64 us (1%)
    pallas_call x1, Pallas kernels, local(): pl.pallas_call(functools.partial(kernel, plan, names, scales), out_shape=...  41.5 us
    pallas_call x1, Pallas kernels, local(): pl.pallas_call(finish, out_shape=[jax.ShapeDtypeStruct(*x) for x in shape...  0.91 us

profile of v6, /device:TPU:1, one launch (start us, length us, event | category | flops | bytes accessed | tf_op | source)
XLA Modules:
  0.0 43.1 jit_solution(17447467492899079573)
XLA Ops:
  0.6 41.5 %step.1 = (bf16[16,16,64]{2,1,0:T(8,128)(2,1)S(1)}, f32[27,4,32]{2,1,0:T(4,128)S(1)}, f32[864,64]{1,0:T(8,128)S(1)}, f32[27,16,64]{2,1,0:T(8,128)S(1)}) custom-call(bf16[4,8,16,512]{3,2,1,0:T(8,128)(2,1)} %refs_0_.1, bf16[27,4,32]{2,1,0:T(4,128)(2,1)} %bitcast.17, bf16[864,64]{1,0:T(8,128)(2,1)} %bitcast.14, bf16[27,16,64]{2,1,0:T(8,128)(2,1)} %bitcast.15, ...), custom_call_target="tpu_custom_call" | custom-call | tf_op jit(solution)/shard_map/step/pallas_call | solution.py:788
  42.2 0.9 %finish.1 = (bf16[16,16,64]{2,1,0:T(8,128)(2,1)}, f32[27,4,32]{2,1,0:T(4,128)}, f32[864,64]{1,0:T(8,128)}, f32[27,16,64]{2,1,0:T(8,128)}) custom-call(bf16[16,16,64]{2,1,0:T(8,128)(2,1)S(1)} %get-tuple-element.12.refs_0_, f32[27,4,32]{2,1,0:T(4,128)S(1)} %get-tuple-element.13.refs_1_, f32[864,64]{1,0:T(8,128)S(1)} %get-tuple-element.14.refs_2_, ...), custom_call_target="tpu_custom_call" | custom-call | tf_op jit(solution)/shard_map/finish/pallas_call | solution.py:799
